TPU v7x, 32 devices: a whole 2x2x4 slice. The times are simulated.
32 devices in a mesh: dp: 8 (over z, x), seq: 4 (over y, core).
Axes of the slice: x: 2, y: 2, z: 4, core: 2. Of those that a mesh axis runs over, the one named last changes fastest.
Arguments:
- layer_in: bfloat16 [16, 256, 768], P('dp', 'seq'), may hold values from -6 to 6
- lengths: int32 [16], P('dp'), may hold values from 64 to 256, as said below
- qkv_weight: bfloat16 [768, 2304], P('dp'), may hold values from -6 to 6
- query_bias: bfloat16 [768], P('dp'), may hold values from -3 to 3
- value_bias: bfloat16 [768], P('dp'), may hold values from -3 to 3
- out_weight: bfloat16 [768, 768], P('dp'), may hold values from -2.5 to 2.5
- out_bias: bfloat16 [768], P('dp'), may hold values from -3 to 3
- attn_gain: bfloat16 [768], P('dp'), may hold values from 0.099609375 to 1.8984375
- attn_shift: bfloat16 [768], P('dp'), may hold values from -3 to 3
- up_weight: bfloat16 [768, 3072], P('dp'), may hold values from -0.21875 to 0.21875
- up_bias: bfloat16 [3072], P('dp'), may hold values from -3 to 3
- down_weight: bfloat16 [3072, 768], P('dp'), may hold values from -0.109375 to 0.109375
- down_bias: bfloat16 [768], P('dp'), may hold values from -3 to 3
- ffn_gain: bfloat16 [768], P('dp'), may hold values from 0.099609375 to 1.8984375
- ffn_shift: bfloat16 [768], P('dp'), may hold values from -3 to 3
- grad_out: bfloat16 [16, 256, 768], P('dp', 'seq'), may hold values from -6 to 6
Outputs:
- layer_out: float32 [16, 256, 768], P('dp', 'seq')
- grad_in: float32 [16, 256, 768], P('dp', 'seq')
- qkv_weight_grad: float32 [768, 2304], P('dp')
- query_bias_grad: float32 [768], P('dp')
- value_bias_grad: float32 [768], P('dp')
- out_weight_grad: float32 [768, 768], P('dp')
- out_bias_grad: float32 [768], P('dp')
- attn_gain_grad: float32 [768], P('dp')
- attn_shift_grad: float32 [768], P('dp')
- up_weight_grad: float32 [768, 3072], P('dp')
- up_bias_grad: float32 [3072], P('dp')
- down_weight_grad: float32 [3072, 768], P('dp')
- down_bias_grad: float32 [768], P('dp')
- ffn_gain_grad: float32 [768], P('dp')
- ffn_shift_grad: float32 [768], P('dp')
Inputs may be any that keep to these rules, and one draw needn't show every extreme that they name: `lengths`: each sequence holds at least 64 real tokens at its start; keys at positions from its length on are padding that no query attends to; in every draw some sequence is 256 long.
All inputs are finite; a program needn't handle non-finite values.
Results may differ from a plain program's by a relative error of at most 0.012.
The roundings to bfloat16 on the way count: a program that leaves them out, or rounds other values in their place, can miss the bound.
Values may be sent and summed in bfloat16 or wider, within the bound.
A program may use at most 128 MiB of HBM per device.

v0:
```python
import math

import jax
import jax.numpy as jnp
from jax import lax
from jax.sharding import PartitionSpec as P

D = 768
H = 12
HD = 64


norm_eps = 1e-12
mask_fill = -1e30


def layer_norm(hidden, gain, shift):
    centred = hidden - jnp.mean(hidden, axis=-1, keepdims=True)
    inverse = lax.rsqrt(jnp.mean(centred * centred, axis=-1, keepdims=True) + norm_eps)
    normed = centred * inverse
    return (normed * gain + shift, normed, inverse)


def norm_back(grad_norm, normed, inverse, gain):
    scaled = grad_norm * gain
    middle = scaled - jnp.mean(scaled, axis=-1, keepdims=True)
    return inverse * (middle - normed * jnp.mean(scaled * normed, axis=-1, keepdims=True))


def gelu_exact(inner):
    return 0.5 * inner * (1.0 + jax.scipy.special.erf(inner * (1.0 / math.sqrt(2.0))))


def gelu_slope(inner):
    cumul = 0.5 * (1.0 + jax.scipy.special.erf(inner * (1.0 / math.sqrt(2.0))))
    return cumul + inner * jnp.exp(-0.5 * inner * inner) * (1.0 / math.sqrt(2.0 * math.pi))


def on_device(
    layer_in,
    lengths,
    qkv_weight,
    query_bias,
    value_bias,
    out_weight,
    out_bias,
    attn_gain,
    attn_shift,
    up_weight,
    up_bias,
    down_weight,
    down_bias,
    ffn_gain,
    ffn_shift,
    grad_out,
):
    params = (
        qkv_weight,
        query_bias,
        value_bias,
        out_weight,
        out_bias,
        attn_gain,
        attn_shift,
        up_weight,
        up_bias,
        down_weight,
        down_bias,
        ffn_gain,
        ffn_shift,
    )
    gathered = (
        lax.all_gather(params[0], "dp", axis=0, tiled=True),
        lax.all_gather(params[1], "dp", axis=0, tiled=True),
        lax.all_gather(params[2], "dp", axis=0, tiled=True),
        lax.all_gather(params[3], "dp", axis=0, tiled=True),
        lax.all_gather(params[4], "dp", axis=0, tiled=True),
        lax.all_gather(params[5], "dp", axis=0, tiled=True),
        lax.all_gather(params[6], "dp", axis=0, tiled=True),
        lax.all_gather(params[7], "dp", axis=0, tiled=True),
        lax.all_gather(params[8], "dp", axis=0, tiled=True),
        lax.all_gather(params[9], "dp", axis=0, tiled=True),
        lax.all_gather(params[10], "dp", axis=0, tiled=True),
        lax.all_gather(params[11], "dp", axis=0, tiled=True),
        lax.all_gather(params[12], "dp", axis=0, tiled=True),
    )
    (
        w_qkv,
        q_bias,
        v_bias,
        w_out,
        b_out,
        gain_raw,
        shift_raw,
        w_up,
        b_up,
        w_down,
        b_down,
        gain_last,
        shift_last,
    ) = gathered
    seqs_here, block, width_model = layer_in.shape
    full_len = block * lax.axis_size("seq")
    rows = seqs_here * block
    pair_width = 2 * HD
    pair_count = H // 2
    score_scale = HD ** (-0.5)
    bias_qkv = jnp.concatenate(
        [q_bias.astype(jnp.float32), jnp.zeros((D,), jnp.float32), v_bias.astype(jnp.float32)]
    )
    gain_one = gain_raw.astype(jnp.float32)
    shift_one = shift_raw.astype(jnp.float32)
    gain_two = gain_last.astype(jnp.float32)
    shift_two = shift_last.astype(jnp.float32)
    tokens = layer_in.reshape(rows, D)
    qkv_proj = (jnp.dot(tokens, w_qkv, preferred_element_type=jnp.float32) + bias_qkv).astype(
        jnp.bfloat16
    )
    qkv_proj = qkv_proj.reshape(seqs_here, block, 3 * D)
    queries = qkv_proj[:, :, :D]
    keys_here = qkv_proj[:, :, D : 2 * D]
    values_here = qkv_proj[:, :, 2 * D :]
    keys_all, values_all = (
        lax.all_gather(keys_here, "seq", axis=1, tiled=True),
        lax.all_gather(values_here, "seq", axis=1, tiled=True),
    )
    valid = jnp.arange(full_len)[None, :] < lengths[:, None]

    def pair_part(array, pair_idx):
        piece = lax.dynamic_slice_in_dim(array, pair_idx * pair_width, pair_width, 2)
        return piece.reshape(piece.shape[:2] + (2, HD))

    def pair_scores(query_pair, key_pair):
        scores = (
            jnp.einsum("sbhd,slhd->shbl", query_pair, key_pair, preferred_element_type=jnp.float32)
            * score_scale
        )
        return jnp.where(valid[:, None, None, :], scores, mask_fill)

    def forward_pair(pair_idx):
        query_pair = pair_part(queries, pair_idx)
        key_pair = pair_part(keys_all, pair_idx)
        value_pair = pair_part(values_all, pair_idx)
        scores = pair_scores(query_pair, key_pair)
        row_top = jnp.max(scores, axis=-1, keepdims=True)
        log_sum = row_top + jnp.log(jnp.sum(jnp.exp(scores - row_top), axis=-1, keepdims=True))
        probs = jnp.exp(scores - log_sum).astype(jnp.bfloat16)
        mixed = jnp.einsum("shbl,slhd->sbhd", probs, value_pair, preferred_element_type=jnp.float32)
        return (mixed.astype(jnp.bfloat16).reshape(seqs_here, block, pair_width), log_sum)

    pair_out, log_sums = lax.map(forward_pair, jnp.arange(pair_count))

    def heads_side(stacked):
        return jnp.transpose(stacked, (1, 2, 0, 3)).reshape(rows, D)

    attended = heads_side(pair_out)
    first_sum = (
        tokens.astype(jnp.float32)
        + jnp.dot(attended, w_out, preferred_element_type=jnp.float32)
        + b_out.astype(jnp.float32)
    )
    first_norm, normed_one, inverse_one = layer_norm(first_sum, gain_one, shift_one)
    first_round = first_norm.astype(jnp.bfloat16)
    inner = jnp.dot(first_round, w_up, preferred_element_type=jnp.float32) + b_up.astype(
        jnp.float32
    )
    activated = gelu_exact(inner).astype(jnp.bfloat16)
    second_sum = (
        first_norm
        + jnp.dot(activated, w_down, preferred_element_type=jnp.float32)
        + b_down.astype(jnp.float32)
    )
    layer_out, normed_two, inverse_two = layer_norm(second_sum, gain_two, shift_two)
    (
        w_qkv,
        q_bias,
        v_bias,
        w_out,
        b_out,
        gain_raw,
        shift_raw,
        w_up,
        b_up,
        w_down,
        b_down,
        gain_last,
        shift_last,
    ) = (
        lax.all_gather(params[0], "dp", axis=0, tiled=True),
        lax.all_gather(params[1], "dp", axis=0, tiled=True),
        lax.all_gather(params[2], "dp", axis=0, tiled=True),
        lax.all_gather(params[3], "dp", axis=0, tiled=True),
        lax.all_gather(params[4], "dp", axis=0, tiled=True),
        lax.all_gather(params[5], "dp", axis=0, tiled=True),
        lax.all_gather(params[6], "dp", axis=0, tiled=True),
        lax.all_gather(params[7], "dp", axis=0, tiled=True),
        lax.all_gather(params[8], "dp", axis=0, tiled=True),
        lax.all_gather(params[9], "dp", axis=0, tiled=True),
        lax.all_gather(params[10], "dp", axis=0, tiled=True),
        lax.all_gather(params[11], "dp", axis=0, tiled=True),
        lax.all_gather(params[12], "dp", axis=0, tiled=True),
    )
    gain_one = gain_raw.astype(jnp.float32)
    gain_two = gain_last.astype(jnp.float32)
    upstream = grad_out.reshape(rows, D).astype(jnp.float32)
    ffn_gain_grad = jnp.sum(upstream * normed_two, axis=0)
    ffn_shift_grad = jnp.sum(upstream, axis=0)
    d_second = norm_back(upstream, normed_two, inverse_two, gain_two)
    d_second_round = d_second.astype(jnp.bfloat16)
    down_weight_grad = jnp.dot(activated.T, d_second_round, preferred_element_type=jnp.float32)
    down_bias_grad = jnp.sum(d_second, axis=0)
    d_inner = jnp.dot(d_second_round, w_down.T, preferred_element_type=jnp.float32) * gelu_slope(
        inner
    )
    d_inner_round = d_inner.astype(jnp.bfloat16)
    up_weight_grad = jnp.dot(first_round.T, d_inner_round, preferred_element_type=jnp.float32)
    up_bias_grad = jnp.sum(d_inner, axis=0)
    d_first_norm = d_second + jnp.dot(d_inner_round, w_up.T, preferred_element_type=jnp.float32)
    attn_gain_grad = jnp.sum(d_first_norm * normed_one, axis=0)
    attn_shift_grad = jnp.sum(d_first_norm, axis=0)
    d_first = norm_back(d_first_norm, normed_one, inverse_one, gain_one)
    d_first_round = d_first.astype(jnp.bfloat16)
    out_weight_grad = jnp.dot(attended.T, d_first_round, preferred_element_type=jnp.float32)
    out_bias_grad = jnp.sum(d_first, axis=0)
    d_attended = jnp.dot(d_first_round, w_out.T, preferred_element_type=jnp.float32).astype(
        jnp.bfloat16
    )
    d_attended = d_attended.reshape(seqs_here, block, D)

    def backward_pair(item):
        pair_idx, log_sum = item
        query_pair = pair_part(queries, pair_idx)
        key_pair = pair_part(keys_all, pair_idx)
        value_pair = pair_part(values_all, pair_idx)
        grad_pair = pair_part(d_attended, pair_idx)
        probs_exact = jnp.exp(pair_scores(query_pair, key_pair) - log_sum)
        d_probs = jnp.einsum(
            "sbhd,slhd->shbl", grad_pair, value_pair, preferred_element_type=jnp.float32
        )
        row_dot = jnp.sum(probs_exact * d_probs, axis=-1, keepdims=True)
        d_scores = (probs_exact * (d_probs - row_dot) * score_scale).astype(jnp.bfloat16)
        probs = probs_exact.astype(jnp.bfloat16)
        d_query = jnp.einsum(
            "shbl,slhd->sbhd", d_scores, key_pair, preferred_element_type=jnp.float32
        )
        d_key = jnp.einsum(
            "shbl,sbhd->slhd", d_scores, query_pair, preferred_element_type=jnp.float32
        )
        d_value = jnp.einsum(
            "shbl,sbhd->slhd", probs, grad_pair, preferred_element_type=jnp.float32
        )
        return (
            d_query.reshape(seqs_here, block, pair_width),
            d_key.reshape(seqs_here, full_len, pair_width),
            d_value.reshape(seqs_here, full_len, pair_width),
        )

    query_pairs, key_pairs, value_pairs = lax.map(backward_pair, (jnp.arange(pair_count), log_sums))
    key_pairs, value_pairs = (
        lax.psum_scatter(key_pairs, "seq", scatter_dimension=2, tiled=True),
        lax.psum_scatter(value_pairs, "seq", scatter_dimension=2, tiled=True),
    )
    d_query = heads_side(query_pairs)
    d_key = heads_side(key_pairs)
    d_value = heads_side(value_pairs)
    d_qkv = jnp.concatenate([d_query, d_key, d_value], axis=1).astype(jnp.bfloat16)
    qkv_weight_grad = jnp.dot(tokens.T, d_qkv, preferred_element_type=jnp.float32)
    query_bias_grad = jnp.sum(d_query, axis=0)
    value_bias_grad = jnp.sum(d_value, axis=0)
    grad_in = d_first + jnp.dot(d_qkv, w_qkv.T, preferred_element_type=jnp.float32)
    grads = (
        qkv_weight_grad,
        query_bias_grad,
        value_bias_grad,
        out_weight_grad,
        out_bias_grad,
        attn_gain_grad,
        attn_shift_grad,
        up_weight_grad,
        up_bias_grad,
        down_weight_grad,
        down_bias_grad,
        ffn_gain_grad,
        ffn_shift_grad,
    )
    owned = (
        lax.psum_scatter(grads[0], "dp", scatter_dimension=0, tiled=True),
        lax.psum_scatter(grads[1], "dp", scatter_dimension=0, tiled=True),
        lax.psum_scatter(grads[2], "dp", scatter_dimension=0, tiled=True),
        lax.psum_scatter(grads[3], "dp", scatter_dimension=0, tiled=True),
        lax.psum_scatter(grads[4], "dp", scatter_dimension=0, tiled=True),
        lax.psum_scatter(grads[5], "dp", scatter_dimension=0, tiled=True),
        lax.psum_scatter(grads[6], "dp", scatter_dimension=0, tiled=True),
        lax.psum_scatter(grads[7], "dp", scatter_dimension=0, tiled=True),
        lax.psum_scatter(grads[8], "dp", scatter_dimension=0, tiled=True),
        lax.psum_scatter(grads[9], "dp", scatter_dimension=0, tiled=True),
        lax.psum_scatter(grads[10], "dp", scatter_dimension=0, tiled=True),
        lax.psum_scatter(grads[11], "dp", scatter_dimension=0, tiled=True),
        lax.psum_scatter(grads[12], "dp", scatter_dimension=0, tiled=True),
    )
    owned = lax.psum(
        (
            owned[0],
            owned[1],
            owned[2],
            owned[3],
            owned[4],
            owned[5],
            owned[6],
            owned[7],
            owned[8],
            owned[9],
            owned[10],
            owned[11],
            owned[12],
        ),
        "seq",
    )
    return (layer_out.reshape(seqs_here, block, D), grad_in.reshape(seqs_here, block, D)) + tuple(
        owned
    )


def solution(mesh):
    in_specs = (
        P("dp", "seq", None),
        P("dp"),
        P("dp", None),
        P("dp"),
        P("dp"),
        P("dp", None),
        P("dp"),
        P("dp"),
        P("dp"),
        P("dp", None),
        P("dp"),
        P("dp", None),
        P("dp"),
        P("dp"),
        P("dp"),
        P("dp", "seq", None),
    )
    out_specs = (
        P("dp", "seq", None),
        P("dp", "seq", None),
        P("dp", None),
        P("dp"),
        P("dp"),
        P("dp", None),
        P("dp"),
        P("dp"),
        P("dp"),
        P("dp", None),
        P("dp"),
        P("dp", None),
        P("dp"),
        P("dp"),
        P("dp"),
    )
    return jax.shard_map(
        on_device, mesh=mesh, in_specs=in_specs, out_specs=out_specs, check_vma=False
    )
```

profile of v0, /device:TPU:0, one launch (start us, length us, event | category | flops | bytes accessed | tf_op | source)
XLA Modules:
  0.0 1091.4 jit_solution(15581011200366759124)
XLA Ops:
  13.4 39.6 %all-reduce.22 = (bf16[768]{0:T(1024)(128)(2,1)S(1)}, bf16[768]{0:T(1024)(128)(2,1)S(1)}, bf16[768]{0:T(1024)(128)(2,1)S(1)}, bf16[768]{0:T(1024)(128)(2,1)S(1)}...) all-reduce(bf16[768]{0:T(1024)(128)(2,1)S(1)} %dynamic-update-slice, ...), channel_id=1, replica_groups=mesh['dp'=8,'seq'=4] {'dp'}, use_global_device_ids=true, to_apply=%add.2 | all-reduce | flops 6144 | bytes 24576
  53.0 26.9 %all-gather = bf16[8,1,384]{2,1,0:T(2,128)(2,1)S(1)} all-gather(bf16[1,1,384]{2,1,0:T(2,128)(2,1)S(1)} %reshape.220), channel_id=1, replica_groups=mesh['dp'=8,'seq'=4] {'dp'}, dimensions={0}, use_global_device_ids=true | all-gather | bytes 6912 | tf_op jit(solution)/shard_map/all_gather | solution.py:81
  80.3 2.7 fusion.29
  83.9 8.6 all_gather.54
  92.5 1.9 copy.73
  94.4 9.0 all_gather.55
  103.4 1.2 copy.74
  104.6 23.7 %while.28 = (s32[]{:T(128)}, bf16[6,2,64,128]{2,3,1,0:T(8,128)(2,1)S(1)}, f32[6,2,2,64,1]{3,2,1,4,0:T(2,128)S(1)}, s32[6]{0:T(128)S(1)}, bf16[2,256,768]{1,2,0:T...) while((s32[]{:T(128)}, ...), condition=%wide.region_3.4_spmd.clone, body=%wide.region_0.3_spmd.clone.sunk | while | flops 17252612 | bytes 1914063 | solution.py:151
  105.8 1.0 constant_dynamic-slice_fusion.13
  109.8 1.0 constant_dynamic-slice_fusion.13
  113.7 1.0 constant_dynamic-slice_fusion.13
  117.7 1.0 constant_dynamic-slice_fusion.13
  121.6 1.0 constant_dynamic-slice_fusion.13
  125.6 1.0 constant_dynamic-slice_fusion.13
  128.6 1.9 fusion.68
  130.7 70.2 %all-gather.10.cloned.1.call-done = bf16[768,3072]{1,0:T(8,128)(2,1)} async-done(((bf16[96,3072]{1,0:T(8,128)(2,1)}), bf16[768,3072]{1,0:T(8,128)(2,1)}) %all-gather.10.cloned.1.call-update) | async-done | bytes 4718608 | tf_op jit(solution)/shard_map/all_gather | solution.py:80
  200.9 3.2 convolution_add_fusion.1
  204.1 76.5 %all-gather.12.cloned.1.call-done = bf16[3072,768]{1,0:T(8,128)(2,1)} async-done(((bf16[384,768]{1,0:T(8,128)(2,1)}), bf16[3072,768]{1,0:T(8,128)(2,1)}) %all-gather.12.cloned.1.call-update) | async-done | bytes 4718608 | tf_op jit(solution)/shard_map/all_gather | solution.py:82
  280.6 3.5 fusion.69
  285.6 1.7 fusion.70
  287.4 1.8 multiply_reduce_fusion.1
  290.6 1.2 convolution_convert_fusion.1
  291.8 48.5 %while.29 = (s32[]{:T(128)}, f32[6,2,64,128]{3,2,0,1:T(8,128)}, f32[6,2,256,128]{3,1,0,2:T(2,128)}, f32[6,2,256,128]{3,1,0,2:T(2,128)}, s32[6]{0:T(128)S(1)}, /*...) while((s32[]{:T(128)}, f32[6,2,64,128]{3,2,0,1:T(8,128)}, ...), condition=%wide.region_14.15_spmd.clone, body=%wide.region_12.14_spmd.clone.sunk | while | flops 42862084 | bytes 6099187 | solution.py:258
  343.5 1.1 bitcast_convert_fusion
  344.7 1.0 bitcast_reduce_fusion
  345.8 35.9 %all-reduce.27.cloned.1.call-done = f32[6,2,256,128]{3,1,0,2:T(2,128)} async-done(((f32[6,2,256,128]{3,1,0,2:T(2,128)}), f32[6,2,256,128]{3,1,0,2:T(2,128)}) %all-reduce.27.cloned.1.call-update) | async-done | bytes 1572880
  381.7 1.1 fusion.47
  382.9 37.5 %all-reduce.19 = (f32[768]{0:T(1024)S(1)}, f32[768]{0:T(1024)S(1)}, f32[768]{0:T(1024)S(1)}, f32[768]{0:T(1024)S(1)}, f32[768]{0:T(1024)S(1)}, /*index=5*/f32[30...) all-reduce(f32[768]{0:T(1024)S(1)} %bitcast.184, ...), channel_id=5, replica_groups=mesh['dp'=8,'seq'=4] {'dp'}, use_global_device_ids=true, to_apply=%region_20.21.clone | all-reduce | flops 9216 | bytes 73728
  421.1 33.6 %all-reduce.30 = (bf16[6,2,256,128]{3,1,0,2:T(2,128)(2,1)}, f32[96]{0:T(128)}, f32[96]{0:T(128)}, f32[96]{0:T(128)}, f32[96]{0:T(128)}, /*index=5*/f32[96]{0:T(1...) all-reduce(f32[6,2,256,128]{3,1,0,2:T(2,128)} %get-tuple-element.12, ...), channel_id=2, replica_groups=mesh['dp'=8,'seq'=4] {'seq'}, use_global_device_ids=true, to_apply=%region_15.16.clone | all-reduce | flops 394368 | bytes 2368512
  454.6 1.1 fusion.49
  455.7 1.1 fusion.48
  457.0 4.0 convolution_bitcast_fusion
  461.0 8.0 copy.85
  470.1 1.9 fusion.50
  472.1 1.1 copy-done.9
  473.2 5.1 fusion.43
  479.3 5.1 fusion.57
  484.5 110.8 %reduce-scatter.13.cloned.1.call-done = f32[96,2304]{1,0:T(8,128)} async-done(((f32[768,2304]{1,0:T(8,128)}), f32[96,2304]{1,0:T(8,128)}) %reduce-scatter.13.cloned.1.call-update) | async-done | bytes 884752
  595.3 2.6 copy.86
  597.8 69.7 %reduce-scatter.7.cloned.1.call-done = f32[96,768]{1,0:T(8,128)} async-done(((f32[768,768]{1,0:T(8,128)}), f32[96,768]{1,0:T(8,128)}) %reduce-scatter.7.cloned.1.call-update) | async-done | bytes 294928 | tf_op jit(solution)/shard_map/reduce_scatter | solution.py:290
  667.5 165.0 %reduce-scatter.9.cloned.1.call-done = f32[96,3072]{1,0:T(8,128)} async-done(((f32[768,3072]{1,0:T(8,128)}), f32[96,3072]{1,0:T(8,128)}) %reduce-scatter.9.cloned.1.call-update) | async-done | bytes 1179664 | tf_op jit(solution)/shard_map/reduce_scatter | solution.py:294
  832.4 164.9 %reduce-scatter.11.cloned.1.call-done = f32[384,768]{1,0:T(8,128)} async-done(((f32[3072,768]{1,0:T(8,128)}), f32[384,768]{1,0:T(8,128)}) %reduce-scatter.11.cloned.1.call-update) | async-done | bytes 1179664 | tf_op jit(solution)/shard_map/reduce_scatter | solution.py:296
  997.3 2.0 copy-done
  999.3 3.2 convolution_add_fusion.3
  1002.5 76.6 %all-reduce.29.cloned.1.call-done = (f32[96,2304]{0,1:T(8,128)}, f32[96,768]{1,0:T(8,128)}, f32[96,3072]{1,0:T(8,128)}, f32[384,768]{1,0:T(8,128)}) async-done(((f32[96,2304]{0,1:T(8,128)}, f32[96,768]{1,0:T(8,128)}, f32[96,3072]{1,0:T(8,128)}, f32[384,768]{1,0:T(8,128)}), (f32[96,2304]{0,1:T(8,128)}, f32[96,768]{1,0:T(8,128)}, f32[96,3072]{1,0:T(8,128)}, ...) | async-done | bytes 3538960 | tf_op jit(solution)/shard_map/psum | solution.py:301
  1079.1 2.7 copy.84
  1082.5 1.0 copy.199
  1083.5 1.0 copy.200
  (321 shorter events, 72.5 us)
Async XLA Ops:
  7.2 3.0 copy-start.17
  7.2 4.3 copy-start.19
  7.2 4.5 copy-start.20
  7.2 4.8 copy-start.21
  7.2 5.0 copy-start.22
  7.2 5.2 copy-start.23
  7.2 5.4 copy-start.24
  7.3 5.7 copy-start.25
  7.3 5.9 copy-start.26
  7.3 45.8 %copy-start.18 = (bf16[384]{0:T(512)(128)(2,1)S(1)}, bf16[384]{0:T(512)(128)(2,1)}, u32[]{:S(2)}) copy-start(bf16[384]{0:T(512)(128)(2,1)} %param.30) | copy-start | bytes 2308
  7.3 72.7 %copy-start.11 = (bf16[2,64,768]{2,1,0:T(8,128)(2,1)S(1)}, bf16[2,64,768]{2,1,0:T(8,128)(2,1)}, u32[]{:S(2)}) copy-start(bf16[2,64,768]{2,1,0:T(8,128)(2,1)} %param.35) | copy-start | bytes 589828
  7.3 73.0 %copy-start.10 = (bf16[2,64,768]{2,1,0:T(8,128)(2,1)S(1)}, bf16[2,64,768]{2,1,0:T(8,128)(2,1)}, u32[]{:S(2)}) copy-start(bf16[2,64,768]{2,1,0:T(8,128)(2,1)} %param.20) | copy-start | bytes 589828
  7.3 73.0 %all-gather.6.cloned.1.call-start = ((), (), s32[]{:S(2)}) async-start(), calls=%async_computation.4 | async-start | bytes 3981312 | tf_op jit(solution)/shard_map/all_gather | solution.py:73
  8.0 120.5 %all-gather.8.cloned.1.call-start = ((), (), s32[]{:S(2)}) async-start(), calls=%async_computation.5 | async-start | bytes 1327104 | tf_op jit(solution)/shard_map/all_gather | solution.py:76
  8.8 192.1 %all-gather.10.cloned.1.call-start = ((), (), s32[]{:S(2)}) async-start(), calls=%async_computation.6 | async-start | bytes 5308416 | tf_op jit(solution)/shard_map/all_gather | solution.py:80
  9.5 271.1 %all-gather.12.cloned.1.call-start = ((), (), s32[]{:S(2)}) async-start(), calls=%async_computation.7 | async-start | bytes 5308416 | tf_op jit(solution)/shard_map/all_gather | solution.py:82
  10.1 371.6 %all-reduce.27.cloned.1.call-start = ((), (), s32[]{:S(2)}) async-start(), calls=%async_computation.12 | async-start | bytes 3145728
  94.4 10.2 copy-start.27
  128.5 75.6 %copy-start.12 = (bf16[2,64,6,128]{3,2,1,0:T(8,128)(2,1)}, bf16[2,64,6,128]{3,2,1,0:T(8,128)(2,1)S(1)}, u32[]{:S(2)}) copy-start(bf16[2,64,6,128]{3,2,1,0:T(8,128)(2,1)S(1)} %copy.75) | copy-start | bytes 589828
  280.6 4.9 copy-start.4
  284.6 2.7 slice-start
  285.6 1.8 copy-start.6
  285.6 1.8 slice-start.1
  287.3 1.9 copy-start.8
  289.2 1.4 copy-start.5
  289.4 0.7 copy-start.1
  340.3 0.7 copy-start.28
  340.4 254.9 %reduce-scatter.13.cloned.1.call-start = ((), (), s32[]{:S(2)}) async-start(), calls=%async_computation.11 | async-start | bytes 7962624
  457.0 4.0 copy-start.3
  469.0 1.0 copy-start.2
  469.0 1.1 copy-start.13
  469.1 198.4 %reduce-scatter.7.cloned.1.call-start = ((), (), s32[]{:S(2)}) async-start(), calls=%async_computation.8 | async-start | bytes 2654208 | tf_op jit(solution)/shard_map/reduce_scatter | solution.py:290
  472.0 1.2 copy-start.9
  472.0 360.4 %reduce-scatter.9.cloned.1.call-start = ((), (), s32[]{:S(2)}) async-start(), calls=%async_computation.9 | async-start | bytes 10616832 | tf_op jit(solution)/shard_map/reduce_scatter | solution.py:294
  478.3 1.0 copy-start.7
  478.3 519.0 %reduce-scatter.11.cloned.1.call-start = ((), (), s32[]{:S(2)}) async-start(), calls=%async_computation.10 | async-start | bytes 10616832 | tf_op jit(solution)/shard_map/reduce_scatter | solution.py:296
  484.4 594.7 %all-reduce.29.cloned.1.call-start = ((), (), s32[]{:S(2)}) async-start(), calls=%async_computation.13 | async-start | bytes 7667712 | tf_op jit(solution)/shard_map/psum | solution.py:301
  997.3 2.0 copy-start
  1079.1 2.7 copy-start.16
  1079.1 3.4 copy-start.15
  1081.8 1.7 copy-start.14
Sparse Core Ops, SparseCore 0:
  10.3 67.9 all-gather.5
  80.5 40.3 all-gather.7
  123.0 77.7 all-gather.9
  202.9 77.6 all-gather.11
  340.5 41.2 all-reduce.26
  469.2 126.0 reduce-scatter.12
  598.8 68.6 reduce-scatter.6
  671.1 161.3 reduce-scatter.8
  836.0 161.2 reduce-scatter.10
  1000.3 78.7 all-reduce.28
where the time goes:
time: 1090 us
  waiting for transfers between devices  772 us (71%)
  blocking collectives  155 us (14%)
  local copies, waits for them, and re-layouts  84.7 us (8%)
  matrix products  45.2 us (4%)
  between operations  17.3 us (2%)
    reduce_scatter x1, waiting for transfers between devices, on_device(): lax.psum_scatter(grads[7], 'dp', scatter_dimension=0, tiled=True)  165 us
    reduce_scatter x1, waiting for transfers between devices, on_device(): lax.psum_scatter(grads[9], 'dp', scatter_dimension=0, tiled=True)  165 us
    unnamed x12, waiting for transfers between devices  149 us
    unnamed x3, blocking collectives  111 us
    psum x1, waiting for transfers between devices, on_device(): lax.psum((owned[0], owned[1], owned[2], owned[3], owned[4], owned[5], own...  76.6 us
    all_gather x1, waiting for transfers between devices, on_device(): lax.all_gather(params[9], 'dp', axis=0, tiled=True)  76.5 us
    all_gather x1, waiting for transfers between devices, on_device(): lax.all_gather(params[7], 'dp', axis=0, tiled=True)  70.2 us
    reduce_scatter x1, waiting for transfers between devices, on_device(): lax.psum_scatter(grads[3], 'dp', scatter_dimension=0, tiled=True)  69.7 us
  transfers between devices with their start and end apart: 10, of which 8 were waited for; matrix products, arithmetic and copies ran while one was open for 5% of the time, Pallas kernels for 0%

commit v1 on v0

--- a/solution.py
+++ b/solution.py
@@ -8,6 +8,7 @@
 D = 768
 H = 12
 HD = 64
+FF = 3072
 
 
 norm_eps = 1e-12
@@ -36,7 +37,7 @@
     return cumul + inner * jnp.exp(-0.5 * inner * inner) * (1.0 / math.sqrt(2.0 * math.pi))
 
 
-def on_device(
+def on_device_general(
     layer_in,
     lengths,
     qkv_weight,
@@ -321,6 +322,227 @@
     )
 
 
+def split_fits(mesh, heads, width, hidden):
+    dp, seq = mesh.shape["dp"], mesh.shape["seq"]
+    return heads % seq == 0 and width % (dp * seq) == 0 and hidden % (dp * seq) == 0
+
+
+def gather_seq(array):
+    return lax.all_gather(array, "seq", axis=1, tiled=True)
+
+
+def scatter_seq(partial):
+    seqs_here, full_len, width = partial.shape
+    count = lax.axis_size("seq")
+    pieces = partial.astype(jnp.bfloat16).reshape(seqs_here, count, full_len // count, width)
+    got = lax.all_to_all(pieces, "seq", 1, 1)
+    return jnp.sum(got.astype(jnp.float32), axis=1)
+
+
+def scatter_dp(grads):
+    return lax.psum_scatter(grads.astype(jnp.bfloat16), "dp", scatter_dimension=0, tiled=True)
+
+
+def on_device(
+    layer_in,
+    lengths,
+    qkv_weight,
+    query_bias,
+    value_bias,
+    out_weight,
+    out_bias,
+    attn_gain,
+    attn_shift,
+    up_weight,
+    up_bias,
+    down_weight,
+    down_bias,
+    ffn_gain,
+    ffn_shift,
+    grad_out,
+):
+    f32, bf16 = jnp.float32, jnp.bfloat16
+    parts, me = lax.axis_size("seq"), lax.axis_index("seq")
+    owners = lax.axis_size("dp")
+    seqs_here, block, width = layer_in.shape
+    full_len = block * parts
+    own = qkv_weight.shape[0]
+    heads = H // parts
+    cols = heads * HD
+    hidden = up_weight.shape[1]
+    unit = hidden // (owners * parts)
+    hidden_part = owners * unit
+    score_scale = HD ** (-0.5)
+
+    def dot(a, b):
+        return jnp.dot(a, b, preferred_element_type=f32)
+
+    def flat(array):
+        return array.reshape(-1, array.shape[-1])
+
+    qkv_mine = lax.dynamic_index_in_dim(
+        qkv_weight.reshape(own, 3, parts, cols), me, 2, keepdims=False
+    ).reshape(own, 3 * cols)
+    up_mine = lax.dynamic_index_in_dim(
+        up_weight.reshape(own, owners, parts, unit), me, 2, keepdims=False
+    ).reshape(own, hidden_part)
+    down_mine = lax.dynamic_slice_in_dim(down_weight, me * unit, unit, 0)
+    up_bias_mine = lax.dynamic_slice_in_dim(up_bias, me * unit, unit, 0)
+    small = jnp.stack(
+        [
+            query_bias,
+            value_bias,
+            out_bias,
+            attn_gain,
+            attn_shift,
+            down_bias,
+            ffn_gain,
+            ffn_shift,
+            up_bias_mine,
+        ],
+        axis=1,
+    )
+    small = jnp.pad(small, ((0, 0), (0, 128 - small.shape[1])))
+    tokens = gather_seq(layer_in)
+    early = lax.all_gather(
+        jnp.concatenate([out_weight, small, qkv_mine], axis=1), "dp", axis=0, tiled=True
+    )
+    late = lax.all_gather(
+        jnp.concatenate([up_mine, down_mine], axis=1), "dp", axis=0, tiled=True
+    )
+    w_out = early[:, :width]
+    vectors = early[:, width : width + 128].T.astype(f32)
+    w_qkv = early[:, width + 128 :]
+    w_up = late[:, :hidden_part]
+    w_down = late[:, hidden_part:]
+    q_bias, v_bias, b_out, gain_one, shift_one, b_down, gain_two, shift_two, b_up = [
+        vectors[k] for k in range(9)
+    ]
+
+    def mine(vector):
+        return lax.dynamic_slice_in_dim(vector, me * cols, cols, 0)
+
+    bias_qkv = jnp.concatenate([mine(q_bias), jnp.zeros((cols,), f32), mine(v_bias)])
+    tokens_flat = flat(tokens)
+    qkv = (dot(tokens_flat, w_qkv) + bias_qkv).astype(bf16)
+    qkv = qkv.reshape(seqs_here, full_len, 3, heads, HD).transpose(2, 0, 3, 1, 4)
+    queries, keys, values = qkv[0], qkv[1], qkv[2]
+    valid = jnp.arange(full_len)[None, :] < lengths[:, None]
+    scores = jnp.einsum("shbd,shld->shbl", queries, keys, preferred_element_type=f32)
+    scores = jnp.where(valid[:, None, None, :], scores * score_scale, mask_fill)
+    row_top = jnp.max(scores, axis=-1, keepdims=True)
+    log_sum = row_top + jnp.log(jnp.sum(jnp.exp(scores - row_top), axis=-1, keepdims=True))
+    probs_exact = jnp.exp(scores - log_sum)
+    probs = probs_exact.astype(bf16)
+    mixed = jnp.einsum("shbl,shld->shbd", probs, values, preferred_element_type=f32)
+    mixed = mixed.astype(bf16).transpose(0, 2, 1, 3).reshape(seqs_here, full_len, cols)
+    attended = lax.all_gather(mixed, "seq", axis=2, tiled=True)
+    attended_flat = flat(attended)
+    first_sum = tokens_flat.astype(f32) + dot(attended_flat, w_out) + b_out
+    first_norm, normed_all, inverse_all = layer_norm(first_sum, gain_one, shift_one)
+
+    def here(rows):
+        rows = rows.reshape(seqs_here, full_len, rows.shape[-1])
+        return flat(lax.dynamic_slice_in_dim(rows, me * block, block, 1))
+
+    normed_one, inverse_one = here(normed_all), here(inverse_all)
+    first_round = first_norm.astype(bf16)
+    inner = dot(first_round, w_up) + b_up
+    activated = gelu_exact(inner).astype(bf16)
+    down = flat(scatter_seq(dot(activated, w_down).reshape(seqs_here, full_len, width)))
+    second_sum = here(first_norm) + down + b_down
+    layer_out, normed_two, inverse_two = layer_norm(second_sum, gain_two, shift_two)
+
+    upstream = flat(grad_out).astype(f32)
+    ffn_gain_grad = jnp.sum(upstream * normed_two, axis=0)
+    ffn_shift_grad = jnp.sum(upstream, axis=0)
+    d_second = norm_back(upstream, normed_two, inverse_two, gain_two)
+    d_second_all = flat(gather_seq(d_second.astype(bf16).reshape(seqs_here, block, width)))
+    down_bias_grad = jnp.sum(d_second, axis=0)
+    d_inner = dot(d_second_all, w_down.T) * gelu_slope(inner)
+    d_inner_round = d_inner.astype(bf16)
+    d_up = flat(scatter_seq(dot(d_inner_round, w_up.T).reshape(seqs_here, full_len, width)))
+    down_weight_grad = dot(activated.T, d_second_all)
+    up_weight_grad = dot(first_round.T, d_inner_round)
+    up_bias_grad = jnp.sum(d_inner, axis=0)
+    late_grads = scatter_dp(jnp.concatenate([up_weight_grad, down_weight_grad], axis=1))
+    d_first_norm = d_second + d_up
+    attn_gain_grad = jnp.sum(d_first_norm * normed_one, axis=0)
+    attn_shift_grad = jnp.sum(d_first_norm, axis=0)
+    d_first = norm_back(d_first_norm, normed_one, inverse_one, gain_one)
+    out_bias_grad = jnp.sum(d_first, axis=0)
+    d_first_all = flat(gather_seq(d_first.astype(bf16).reshape(seqs_here, block, width)))
+    out_weight_grad = dot(
+        attended_flat.T, lax.dynamic_slice_in_dim(d_first_all, me * cols, cols, 1)
+    )
+    w_out_mine = lax.dynamic_slice_in_dim(w_out, me * cols, cols, 0)
+    d_attended = dot(d_first_all, w_out_mine.T).astype(bf16)
+    d_attended = d_attended.reshape(seqs_here, full_len, heads, HD).transpose(0, 2, 1, 3)
+    d_probs = jnp.einsum("shbd,shld->shbl", d_attended, values, preferred_element_type=f32)
+    row_dot = jnp.sum(probs_exact * d_probs, axis=-1, keepdims=True)
+    d_scores = (probs_exact * (d_probs - row_dot) * score_scale).astype(bf16)
+    d_query = jnp.einsum("shbl,shld->shbd", d_scores, keys, preferred_element_type=f32)
+    d_key = jnp.einsum("shbl,shbd->shld", d_scores, queries, preferred_element_type=f32)
+    d_value = jnp.einsum("shbl,shbd->shld", probs, d_attended, preferred_element_type=f32)
+    query_bias_grad = jnp.sum(d_query, axis=(0, 2)).reshape(cols)
+    value_bias_grad = jnp.sum(d_value, axis=(0, 2)).reshape(cols)
+    d_qkv = jnp.stack([d_query, d_key, d_value]).astype(bf16)
+    d_qkv = d_qkv.transpose(1, 3, 0, 2, 4).reshape(seqs_here * full_len, 3 * cols)
+    qkv_weight_grad = dot(tokens_flat.T, d_qkv)
+
+    def placed(vector):
+        return lax.dynamic_update_slice_in_dim(jnp.zeros((width,), f32), vector, me * cols, 0)
+
+    small_grads = jnp.stack(
+        [
+            placed(query_bias_grad),
+            placed(value_bias_grad),
+            out_bias_grad,
+            attn_gain_grad,
+            attn_shift_grad,
+            down_bias_grad,
+            ffn_gain_grad,
+            ffn_shift_grad,
+            up_bias_grad,
+        ]
+    )
+    small_grads = jnp.pad(small_grads, ((0, 128 - small_grads.shape[0]), (0, 0))).T
+    early_grads = scatter_dp(
+        jnp.concatenate([small_grads, qkv_weight_grad, out_weight_grad], axis=1)
+    )
+    d_in = flat(scatter_seq(dot(d_qkv, w_qkv.T).reshape(seqs_here, full_len, width)))
+    grad_in = d_first + d_in
+
+    late_all = lax.all_gather(late_grads, "seq", axis=0)
+    early_all = lax.all_gather(early_grads, "seq", axis=0)
+    up_owned = late_all[:, :, :hidden_part].reshape(parts, own, owners, unit)
+    up_owned = up_owned.transpose(1, 2, 0, 3).reshape(own, hidden).astype(f32)
+    down_owned = late_all[:, :, hidden_part:].reshape(parts * unit, width).astype(f32)
+    small_owned = early_all[:, :, :128].astype(f32)
+    sums = jnp.sum(small_owned, axis=0).T
+    up_bias_owned = small_owned[:, :, 8].reshape(parts * unit)
+    qkv_owned = early_all[:, :, 128 : 128 + 3 * cols].reshape(parts, own, 3, cols)
+    qkv_owned = qkv_owned.transpose(1, 2, 0, 3).reshape(own, 3 * width).astype(f32)
+    out_owned = early_all[:, :, 128 + 3 * cols :].transpose(1, 0, 2).reshape(own, width)
+    return (
+        layer_out.reshape(seqs_here, block, width),
+        grad_in.reshape(seqs_here, block, width),
+        qkv_owned,
+        sums[0],
+        sums[1],
+        out_owned.astype(f32),
+        sums[2],
+        sums[3],
+        sums[4],
+        up_owned,
+        up_bias_owned,
+        down_owned,
+        sums[5],
+        sums[6],
+        sums[7],
+    )
+
+
 def solution(mesh):
     in_specs = (
         P("dp", "seq", None),
@@ -357,6 +579,7 @@
         P("dp"),
         P("dp"),
     )
+    body = on_device if split_fits(mesh, H, D, FF) else on_device_general
     return jax.shard_map(
-        on_device, mesh=mesh, in_specs=in_specs, out_specs=out_specs, check_vma=False
-    )
+        body, mesh=mesh, in_specs=in_specs, out_specs=out_specs, check_vma=False
+    )

time: 1090 us -> 334 us (0.31)
  waiting for transfers between devices: 772 us -> 171 us
  blocking collectives: 155 us -> 43.8 us
  local copies, waits for them, and re-layouts: 84.7 us -> 44.3 us
  matrix products: 45.2 us -> 28.8 us
  other arithmetic: 7.37 us -> 19.5 us
    reduce_scatter x3 -> x2, waiting for transfers between devices: 399 us -> 79.5 us  [scatter_dp(): lax.psum_scatter(grads.astype(jnp.bfloat16), 'dp', scatter_dimension=0, t...]
    unnamed x12 -> x5, waiting for transfers between devices: 149 us -> 0.08 us
    unnamed x3 -> x0, blocking collectives: 111 us -> none
    psum x1 -> x0, waiting for transfers between devices: 76.6 us -> none  [on_device(): lax.psum((owned[0], owned[1], owned[2], owned[3], owned[4], owned[5], own...]
    all_gather x4 -> x3, waiting for transfers between devices: 147 us -> 74.5 us  [the longest x1 41.4 us: on_device(): lax.all_gather(jnp.concatenate([out_weight, small, qkv_mine], axis=1), 'd...]
    dynamic_slice x48 -> x5, local copies, waits for them, and re-layouts: 37.9 us -> 1.81 us  [the longest x1 1.25 us: on_device(): lax.dynamic_index_in_dim(up_weight.reshape(own, owners, parts, unit), me,...]
    unnamed x101 -> x91, local copies, waits for them, and re-layouts: 29.6 us -> 10.8 us
    all_to_all x0 -> x3, waiting for transfers between devices: none -> 16.9 us  [scatter_seq(): got = lax.all_to_all(pieces, 'seq', 1, 1)]
  transfers between devices with their start and end apart: 10 -> 8, of which waited for: 8 -> 7; matrix products, arithmetic and copies ran while one was open for 5% -> 17% of each run, Pallas kernels for 0% -> 0%
where the time goes in v1:
time: 334 us; the launch traced here: 333 us
  waiting for transfers between devices  171 us (51%)
  local copies, waits for them, and re-layouts  44.3 us (13%)
  blocking collectives  43.8 us (13%)
  matrix products  28.8 us (9%)
  other arithmetic  19.5 us (6%)
  between operations  14.5 us (4%)
  starting transfers between devices  10.7 us (3%)
    reduce_scatter x2, waiting for transfers between devices, scatter_dp(): lax.psum_scatter(grads.astype(jnp.bfloat16), 'dp', scatter_dimension=0, t...  79.5 us
    all_gather x1, waiting for transfers between devices, on_device(): lax.all_gather(jnp.concatenate([out_weight, small, qkv_mine], axis=1), 'd...  41.4 us
    all_gather x1, waiting for transfers between devices, on_device(): lax.all_gather(jnp.concatenate([up_mine, down_mine], axis=1), 'dp', axis=...  30.7 us
    all_gather x3, blocking collectives, gather_seq(): return lax.all_gather(array, 'seq', axis=1, tiled=True)  26.3 us
    dot_general x12, matrix products, dot(): return jnp.dot(a, b, preferred_element_type=f32)  17.8 us
    all_to_all x3, waiting for transfers between devices, scatter_seq(): got = lax.all_to_all(pieces, 'seq', 1, 1)  16.9 us
    unnamed x91, local copies, waits for them, and re-layouts  10.8 us
    all_to_all x3, starting transfers between devices, scatter_seq(): got = lax.all_to_all(pieces, 'seq', 1, 1)  10.5 us
  transfers between devices with their start and end apart: 8, of which 7 were waited for; matrix products, arithmetic and copies ran while one was open for 17% of the time, Pallas kernels for 0%

profile of v1, /device:TPU:0, one launch (start us, length us, event | category | flops | bytes accessed | tf_op | source)
XLA Modules:
  0.0 332.8 jit_solution(16540723296354407424)
XLA Ops:
  9.0 1.7 reshape.702
  13.0 1.2 dynamic-slice_reduce_fusion
  15.3 10.1 %all_gather.30 = bf16[2,256,768]{2,1,0:T(8,128)(2,1)S(1)} all-gather(bf16[2,64,768]{2,1,0:T(8,128)(2,1)S(1)} %copy-done.14), channel_id=1, replica_groups=mesh['dp'=8,'seq'=4] {'seq'}, dimensions={1}, use_global_device_ids=true | all-gather | bytes 983040 | tf_op jit(solution)/shard_map/all_gather | solution.py:331
  25.4 41.4 %all-gather.6.cloned.1.call-done = bf16[768,1472]{1,0:T(8,128)(2,1)} async-done(((bf16[96,1472]{1,0:T(8,128)(2,1)}), bf16[768,1472]{1,0:T(8,128)(2,1)}) %all-gather.6.cloned.1.call-update) | async-done | bytes 2261008 | tf_op jit(solution)/shard_map/all_gather | solution.py:407
  67.8 2.2 slice_reduce_fusion.1
  72.6 9.0 %all_gather.32 = bf16[2,256,768]{1,0,2:T(2,128)(2,1)} all-gather(bf16[2,256,192]{1,0,2:T(2,128)(2,1)S(1)} %copy.124), channel_id=1, replica_groups=mesh['dp'=8,'seq'=4] {'seq'}, dimensions={2}, use_global_device_ids=true | all-gather | bytes 983040 | tf_op jit(solution)/shard_map/all_gather | solution.py:439
  81.7 2.2 copy.125
  83.9 2.7 fusion.82
  87.3 2.0 multiply_add_fusion
  89.3 30.7 %all-gather.8.cloned.1.call-done = bf16[768,1536]{1,0:T(8,128)(2,1)} async-done(((bf16[96,1536]{1,0:T(8,128)(2,1)}), bf16[768,1536]{1,0:T(8,128)(2,1)}) %all-gather.8.cloned.1.call-update) | async-done | bytes 2359312 | tf_op jit(solution)/shard_map/all_gather | solution.py:410
  120.0 3.9 %multiply_convert_fusion.1 = (bf16[512,768]{1,0:T(8,128)(2,1)S(1)}, f32[512,768]{1,0:T(8,128)}) fusion(f32[768]{0:T(1024)S(1)} %copy-done.32, bf16[768,1536]{1,0:T(8,128)(2,1)} %all-gather.8.cloned.1.call-done, f32[512,768]{1,0:T(8,128)} %get-tuple-element.43), kind=kOutput, calls=%fused_computation.14 | convolution fusion | flops 606732288 | bytes 5114880 | tf_op jit(solution)/shard_map/dot_general | solution.py:378
  125.8 3.5 %all-to-all-start = ((bf16[2,4,64,768]{3,2,0,1:T(8,128)(2,1)}), bf16[2,4,64,768]{3,2,0,1:T(8,128)(2,1)S(1)}, u32[]{:S(2)}, u32[]{:S(2)}) async-start(bf16[2,4,64,768]{3,2,0,1:T(8,128)(2,1)} %copy.127), calls=%async_computation | async-start | bytes 1572864 | tf_op jit(solution)/shard_map/all_to_all | solution.py:338
  129.3 11.5 %all-to-all-done = bf16[2,4,64,768]{3,2,0,1:T(8,128)(2,1)S(1)} async-done(((bf16[2,4,64,768]{3,2,0,1:T(8,128)(2,1)}), bf16[2,4,64,768]{3,2,0,1:T(8,128)(2,1)S(1)}, u32[]{:S(2)}, u32[]{:S(2)}) %all-to-all-start) | async-done | bytes 786464 | tf_op jit(solution)/shard_map/all_to_all | solution.py:338
  141.0 1.1 fusion.77
  142.6 1.6 fusion.46
  144.2 8.2 %all_gather.34 = bf16[2,256,768]{2,1,0:T(8,128)(2,1)S(1)} all-gather(bf16[2,64,768]{2,1,0:T(8,128)(2,1)S(1)} %get-tuple-element.47), channel_id=1, replica_groups=mesh['dp'=8,'seq'=4] {'seq'}, dimensions={1}, use_global_device_ids=true | all-gather | bytes 983040 | tf_op jit(solution)/shard_map/all_gather | solution.py:331
  154.1 1.7 fusion.83
  156.6 1.6 pad_maximum_fusion
  158.2 4.3 %copy.148 = bf16[768,1536]{1,0:T(8,128)(2,1)} copy(bf16[768,1536]{0,1:T(8,128)(2,1)} %pad_maximum_fusion) | data formatting | bytes 4718592
  162.5 2.1 convolution_convert_fusion.3
  165.5 3.6 %all-to-all-start.1 = ((bf16[2,4,64,768]{3,2,0,1:T(8,128)(2,1)}), bf16[2,4,64,768]{3,2,0,1:T(8,128)(2,1)S(1)}, u32[]{:S(2)}, u32[]{:S(2)}) async-start(bf16[2,4,64,768]{3,2,0,1:T(8,128)(2,1)} %copy.128), calls=%async_computation.1 | async-start | bytes 1572864 | tf_op jit(solution)/shard_map/all_to_all | solution.py:338
  169.8 1.3 stack.108
  171.0 1.3 rsqrt.28
  175.3 5.3 %all-to-all-done.1 = bf16[2,4,64,768]{3,2,0,1:T(8,128)(2,1)S(1)} async-done(((bf16[2,4,64,768]{3,2,0,1:T(8,128)(2,1)}), bf16[2,4,64,768]{3,2,0,1:T(8,128)(2,1)S(1)}, u32[]{:S(2)}, u32[]{:S(2)}) %all-to-all-start.1) | async-done | bytes 786464 | tf_op jit(solution)/shard_map/all_to_all | solution.py:338
  180.8 2.0 multiply_reduce_fusion.2
  182.8 1.3 fusion.75
  184.1 8.0 %all_gather.35 = bf16[2,256,768]{2,1,0:T(8,128)(2,1)S(1)} all-gather(bf16[2,64,768]{2,1,0:T(8,128)(2,1)S(1)} %convert_element_type.158), channel_id=1, replica_groups=mesh['dp'=8,'seq'=4] {'seq'}, dimensions={1}, use_global_device_ids=true | all-gather | bytes 983040 | tf_op jit(solution)/shard_map/all_gather | solution.py:331
  192.1 1.1 convolution_convert_fusion.8
  193.2 1.0 reshape.713
  194.1 1.6 fusion.59
  195.7 3.4 %fusion.21 = bf16[1,2,3,256,64]{3,4,2,1,0:T(8,128)(2,1)} fusion(f32[2,3,256,256]{2,3,1,0:T(8,128)} %fusion.59, f32[2,3,256,256]{2,3,1,0:T(8,128)S(1)} %get-tuple-element.56, f32[2,3,256]{2,1,0:T(4,128)S(1)} %log_add_fusion, bf16[3,2,3,256,64]{3,4,2,1,0:T(8,128)(2,1)S(1)} %bitcast.123), kind=kOutput, calls=%fused_computation.41 | convolution fusion | flops 53184256 | bytes 6701056 | tf_op jit(solution)/shard_map/shbl,shbd->shld/dot_general | solution.py:485
  199.1 1.1 fusion.55
  200.2 4.2 %fusion.79 = (bf16[3,64]{1,0:T(4,128)(2,1)S(1)}, bf16[1,2,3,256,64]{3,4,2,1,0:T(8,128)(2,1)}, bf16[1,2,3,256,64]{3,4,2,1,0:T(8,128)(2,1)}, bf16[3,64]{1,0:T(4,128)(2,1)}) fusion(f32[2,3,256,64]{2,3,1,0:T(8,128)} %fusion.55, f32[2,3,256,256]{2,3,1,0:T(8,128)} %fusion.59, f32[2,3,256,256]{2,3,1,0:T(8,128)S(1)} %get-tuple-element.56, ...), kind=kOutput, calls=%fused_computation.153 | convolution fusion | flops 53478784 | bytes 7291648 | tf_op jit(solution)/shard_map/shbl,shld->shbd/dot_general | solution.py:484
  204.5 1.1 maximum_bitcast_fusion
  207.5 1.8 fusion.16
  209.4 1.6 copy.146
  211.1 1.6 copy-done.10
  214.5 3.5 %all-to-all-start.2 = ((bf16[2,4,64,768]{3,2,0,1:T(8,128)(2,1)}), bf16[2,4,64,768]{3,2,0,1:T(8,128)(2,1)S(1)}, u32[]{:S(2)}, u32[]{:S(2)}) async-start(bf16[2,4,64,768]{3,2,0,1:T(8,128)(2,1)} %copy.134), calls=%async_computation.2 | async-start | bytes 1572864 | tf_op jit(solution)/shard_map/all_to_all | solution.py:338
  218.0 12.5 %reduce-scatter.9.cloned.1.call-done = bf16[96,1536]{1,0:T(8,128)(2,1)} async-done(((bf16[768,1536]{1,0:T(8,128)(2,1)}), bf16[96,1536]{1,0:T(8,128)(2,1)}) %reduce-scatter.9.cloned.1.call-update) | async-done | bytes 294928 | tf_op jit(solution)/shard_map/reduce_scatter | solution.py:343
  231.5 66.9 %reduce-scatter.7.cloned.1.call-done = bf16[96,896]{1,0:T(8,128)(2,1)} async-done(((bf16[768,896]{1,0:T(8,128)(2,1)}), bf16[96,896]{1,0:T(8,128)(2,1)}) %reduce-scatter.7.cloned.1.call-update) | async-done | bytes 172048 | tf_op jit(solution)/shard_map/reduce_scatter | solution.py:343
  298.4 8.5 %all-gather = bf16[384,896]{1,0:T(8,128)(2,1)S(1)} all-gather(bf16[96,896]{1,0:T(8,128)(2,1)} %reduce-scatter.7.cloned.1.call-done), channel_id=2, replica_groups=mesh['dp'=8,'seq'=4] {'seq'}, dimensions={0}, use_global_device_ids=true | all-gather | bytes 860160 | tf_op jit(solution)/shard_map/all_gather | solution.py:517
  309.2 1.7 reshape.716
  311.2 1.0 reshape.717
  314.0 2.3 all-gather.10.cloned.1.call-done
  316.3 2.2 fusion.78
  319.2 2.2 copy.141
  321.4 3.7 %reshape.718 = f32[96,3072]{1,0:T(8,128)} reshape(f32[96,8,4,96]{3,2,1,0:T(4,128)} %copy.141) | data formatting | bytes 2359296 | tf_op jit(solution)/shard_map/convert_element_type | solution.py:519
  325.1 1.1 bitcast_convert_fusion
  (178 shorter events, 28.7 us)
Async XLA Ops:
  7.2 7.3 %copy-start = (bf16[384,768]{1,0:T(8,128)(2,1)S(1)}, bf16[384,768]{1,0:T(8,128)(2,1)}, u32[]{:S(2)}) copy-start(bf16[384,768]{1,0:T(8,128)(2,1)} %param.27) | copy-start | bytes 1769476
  7.2 4.2 %copy-start.15 = (bf16[96,768]{1,0:T(8,128)(2,1)S(1)}, bf16[96,768]{1,0:T(8,128)(2,1)}, u32[]{:S(2)}) copy-start(bf16[96,768]{1,0:T(8,128)(2,1)} %param.21) | copy-start | bytes 442372
  7.2 59.7 %all-gather.6.cloned.1.call-start = ((), (), s32[]{:S(2)}) async-start(), calls=%async_computation.5 | async-start | bytes 2654208 | tf_op jit(solution)/shard_map/all_gather | solution.py:407
  9.0 3.2 copy-start.12
  12.2 3.1 copy-start.39
  12.2 3.2 copy-start.14
  12.2 107.8 %all-gather.8.cloned.1.call-start = ((), (), s32[]{:S(2)}) async-start(), calls=%async_computation.6 | async-start | bytes 2654208 | tf_op jit(solution)/shard_map/all_gather | solution.py:410
  25.4 44.9 %copy-start.11 = (bf16[2,256,768]{2,1,0:T(8,128)(2,1)}, bf16[2,256,768]{2,1,0:T(8,128)(2,1)S(1)}, u32[]{:S(2)}) copy-start(bf16[2,256,768]{2,1,0:T(8,128)(2,1)S(1)} %all_gather.30) | copy-start | bytes 2359300
  67.8 2.5 copy-start.9
  72.4 11.5 %copy-start.33 = (f32[768]{0:T(1024)S(1)}, f32[768]{0:T(1024)}, u32[]{:S(2)}) copy-start(f32[768]{0:T(1024)} %get-tuple-element.27) | copy-start | bytes 9220
  83.9 2.7 copy-start.5
  86.9 2.3 copy-start.17
  87.3 32.7 %copy-start.32 = (f32[768]{0:T(1024)S(1)}, f32[768]{0:T(1024)}, u32[]{:S(2)}) copy-start(f32[768]{0:T(1024)} %get-tuple-element.24) | copy-start | bytes 9220
  120.0 4.0 %copy-start.37 = (bf16[768,1536]{1,0:T(8,128)(2,1)S(1)}, bf16[768,1536]{1,0:T(8,128)(2,1)}, u32[]{:S(2)}) copy-start(bf16[768,1536]{1,0:T(8,128)(2,1)} %all-gather.8.cloned.1.call-done) | copy-start | bytes 7077892
  125.8 15.1 %all-to-all-start = ((bf16[2,4,64,768]{3,2,0,1:T(8,128)(2,1)}), bf16[2,4,64,768]{3,2,0,1:T(8,128)(2,1)S(1)}, u32[]{:S(2)}, u32[]{:S(2)}) async-start(bf16[2,4,64,768]{3,2,0,1:T(8,128)(2,1)} %copy.127), calls=%async_computation | async-start | bytes 1572864 | tf_op jit(solution)/shard_map/all_to_all | solution.py:338
  129.3 13.1 %copy-start.7 = (bf16[2,64,768]{2,1,0:T(8,128)(2,1)S(1)}, bf16[2,64,768]{2,1,0:T(8,128)(2,1)}, u32[]{:S(2)}) copy-start(bf16[2,64,768]{2,1,0:T(8,128)(2,1)} %param.31) | copy-start | bytes 589828
  129.3 101.3 %reduce-scatter.9.cloned.1.call-start = ((), (), s32[]{:S(2)}) async-start(), calls=%async_computation.9 | async-start | bytes 2654208 | tf_op jit(solution)/shard_map/reduce_scatter | solution.py:343
  140.9 1.8 copy-start.18
  142.1 10.3 %copy-start.16 = (f32[2,64]{1,0:T(2,128)}, f32[2,64]{1,0:T(2,128)S(1)}, u32[]{:S(2)}) copy-start(f32[2,64]{1,0:T(2,128)S(1)} %broadcast_multiply_fusion.5) | copy-start | bytes 1540
  142.1 10.3 %copy-start.42 = (bf16[512,768]{1,0:T(8,128)(2,1)S(1)}, bf16[512,768]{1,0:T(8,128)(2,1)}, u32[]{:S(2)}) copy-start(bf16[512,768]{1,0:T(8,128)(2,1)} %copy-done.41) | copy-start | bytes 2359300
  142.3 10.9 %copy-start.19 = (f32[2,64]{1,0:T(2,128)}, f32[2,64]{1,0:T(2,128)S(1)}, u32[]{:S(2)}) copy-start(f32[2,64]{1,0:T(2,128)S(1)} %add_rsqrt_fusion.1) | copy-start | bytes 1540
  142.6 10.7 %copy-start.25 = (f32[2,64]{1,0:T(2,128)}, f32[2,64]{1,0:T(2,128)S(1)}, u32[]{:S(2)}) copy-start(f32[2,64]{1,0:T(2,128)S(1)} %broadcast_multiply_fusion.3) | copy-start | bytes 1540
  142.6 10.6 %copy-start.26 = (f32[2,64]{1,0:T(2,128)}, f32[2,64]{1,0:T(2,128)S(1)}, u32[]{:S(2)}) copy-start(f32[2,64]{1,0:T(2,128)S(1)} %broadcast_multiply_fusion.4) | copy-start | bytes 1540
  144.2 9.1 %copy-start.40 = (f32[512,768]{1,0:T(8,128)S(1)}, f32[512,768]{1,0:T(8,128)}, u32[]{:S(2)}) copy-start(f32[512,768]{1,0:T(8,128)} %get-tuple-element.60) | copy-start | bytes 4718596
  152.4 1.7 copy-start.38
  154.1 1.7 copy-start.2
  165.5 15.1 %all-to-all-start.1 = ((bf16[2,4,64,768]{3,2,0,1:T(8,128)(2,1)}), bf16[2,4,64,768]{3,2,0,1:T(8,128)(2,1)S(1)}, u32[]{:S(2)}, u32[]{:S(2)}) async-start(bf16[2,4,64,768]{3,2,0,1:T(8,128)(2,1)} %copy.128), calls=%async_computation.1 | async-start | bytes 1572864 | tf_op jit(solution)/shard_map/all_to_all | solution.py:338
  169.1 129.4 %reduce-scatter.7.cloned.1.call-start = ((), (), s32[]{:S(2)}) async-start(), calls=%async_computation.8 | async-start | bytes 1548288 | tf_op jit(solution)/shard_map/reduce_scatter | solution.py:343
  172.3 1.3 copy-start.30
  172.3 1.9 copy-start.29
  172.3 2.5 copy-start.35
  180.7 2.1 copy-start.34
  182.8 9.3 %slice-start = ((bf16[768,1472]{1,0:T(8,128)(2,1)}), bf16[768,768]{1,0:T(8,128)(2,1)S(1)}, s32[]{:S(2)}) async-start(bf16[768,1472]{1,0:T(8,128)(2,1)} %all-gather.6.cloned.1.call-done), calls=%async_computation.10 | async-start | bytes 2359296 | tf_op jit(solution)/shard_map/slice | solution.py:413
  200.2 4.2 %copy-start.13 = (bf16[1,2,3,256,64]{3,4,2,1,0:T(8,128)(2,1)S(1)}, bf16[1,2,3,256,64]{3,4,2,1,0:T(8,128)(2,1)}, u32[]{:S(2)}) copy-start(bf16[1,2,3,256,64]{3,4,2,1,0:T(8,128)(2,1)} %fusion.21) | copy-start | bytes 589828
  204.4 1.9 copy-start.36
  204.4 2.1 copy-start.28
  204.4 2.1 copy-start.27
  204.4 2.5 copy-start.21
  204.5 2.5 copy-start.22
  204.5 2.5 copy-start.23
  204.5 2.5 copy-start.24
  205.6 1.5 copy-start.6
  211.0 1.7 copy-start.10
  214.5 16.1 %all-to-all-start.2 = ((bf16[2,4,64,768]{3,2,0,1:T(8,128)(2,1)}), bf16[2,4,64,768]{3,2,0,1:T(8,128)(2,1)S(1)}, u32[]{:S(2)}, u32[]{:S(2)}) async-start(bf16[2,4,64,768]{3,2,0,1:T(8,128)(2,1)} %copy.134), calls=%async_computation.2 | async-start | bytes 1572864 | tf_op jit(solution)/shard_map/all_to_all | solution.py:338
  218.0 98.4 %all-gather.10.cloned.1.call-start = ((), (), s32[]{:S(2)}) async-start(), calls=%async_computation.7 | async-start | bytes 1474560 | tf_op jit(solution)/shard_map/all_gather | solution.py:516
  309.1 1.7 copy-start.4
  321.4 3.7 %copy-start.8 = (bf16[4,96,768]{2,1,0:T(8,128)(2,1)S(1)}, bf16[4,96,768]{2,1,0:T(8,128)(2,1)}, u32[]{:S(2)}) copy-start(bf16[4,96,768]{2,1,0:T(8,128)(2,1)} %get-tuple-element.45) | copy-start | bytes 1769476
  321.4 4.8 %copy-start.1 = (bf16[384,768]{1,0:T(8,128)(2,1)S(1)}, bf16[384,768]{1,0:T(8,128)(2,1)}, u32[]{:S(2)}) copy-start(bf16[384,768]{1,0:T(8,128)(2,1)} %param.27) | copy-start | bytes 1769476
  (4 other events, 3.1 us)
Sparse Core Ops, SparseCore 0:
  12.3 54.5 all-gather.5
  69.6 50.3 all-gather.7
  162.6 67.8 reduce-scatter.8
  233.8 64.5 reduce-scatter.6
  299.9 16.4 all-gather.9

commit v2 on v1

--- a/solution.py
+++ b/solution.py
@@ -1,8 +1,11 @@
+import functools
 import math
 
 import jax
 import jax.numpy as jnp
 from jax import lax
+from jax.experimental import pallas as pl
+from jax.experimental.pallas import tpu as pltpu
 from jax.sharding import PartitionSpec as P
 
 D = 768
@@ -324,7 +327,196 @@
 
 def split_fits(mesh, heads, width, hidden):
     dp, seq = mesh.shape["dp"], mesh.shape["seq"]
-    return heads % seq == 0 and width % (dp * seq) == 0 and hidden % (dp * seq) == 0
+    return heads % seq == 0 and dp % 2 == 0 and width % (dp * seq) == 0 and hidden % (dp * seq) == 0
+
+
+def remote(src, dst, send_sem, recv_sem, peer):
+    copy = pltpu.make_async_remote_copy(
+        src_ref=src,
+        dst_ref=dst,
+        send_sem=send_sem,
+        recv_sem=recv_sem,
+        device_id=peer,
+        device_id_type=pl.DeviceIdType.MESH,
+    )
+    copy.start()
+    return copy
+
+
+def greet(peers):
+    barrier = pltpu.get_barrier_semaphore()
+    for peer in peers:
+        pl.semaphore_signal(
+            barrier, inc=1, device_id=peer, device_id_type=pl.DeviceIdType.MESH
+        )
+    pl.semaphore_wait(barrier, len(peers))
+
+
+def places(owners, parts):
+    at = lax.axis_index("dp")
+    line, side = at // 2, at % 2
+    lines = owners // 2
+    me = lax.axis_index("seq")
+    line_peers = [{"dp": ((line + k) % lines) * 2 + side} for k in range(1, lines)]
+    seq_peers = [{"seq": (me + k) % parts} for k in range(1, parts)]
+    return line, side, lines, me, line_peers, {"dp": line * 2 + 1 - side}, seq_peers
+
+
+def start_kernel(
+    owners, parts, x_ref, w_ref, x_out, w_out, x_send, x_recv, l_send, l_recv, p_send, p_recv
+):
+    line, side, lines, me, line_peers, pair, seq_peers = places(owners, parts)
+    greet(line_peers + [pair] + seq_peers)
+    block = x_ref.shape[1]
+    mine = line * 2 + side
+    rows = pl.ds(pl.multiple_of(me * block, block), block)
+    copies = []
+    for k, peer in enumerate(line_peers):
+        copies.append(remote(w_ref, w_out.at[mine], l_send.at[k], l_recv.at[k], peer))
+    paired = [remote(w_ref, w_out.at[mine], p_send.at[0], p_recv.at[0], pair)]
+    tokens = []
+    for k, peer in enumerate(seq_peers):
+        tokens.append(remote(x_ref, x_out.at[:, rows, :], x_send.at[k], x_recv.at[k], peer))
+    w_out[mine] = w_ref[...]
+    x_out[:, rows, :] = x_ref[...]
+    for k in range(1, lines):
+        copies[k - 1].wait_recv()
+        slot = w_out.at[((line + lines - k) % lines) * 2 + side]
+        paired.append(remote(slot, slot, p_send.at[k], p_recv.at[k], pair))
+    for copy in copies:
+        copy.wait_send()
+    for copy in paired + tokens:
+        copy.wait()
+
+
+def gather_start(layer_in, weights, owners, parts):
+    seqs_here, block, width = layer_in.shape
+    own, cols = weights.shape
+    vmem = pl.BlockSpec(memory_space=pltpu.VMEM)
+    dma = pltpu.SemaphoreType.DMA
+    lines = owners // 2
+    return pl.pallas_call(
+        functools.partial(start_kernel, owners, parts),
+        out_shape=(
+            jax.ShapeDtypeStruct((seqs_here, block * parts, width), layer_in.dtype),
+            jax.ShapeDtypeStruct((owners, own, cols), weights.dtype),
+        ),
+        in_specs=[vmem, vmem],
+        out_specs=(vmem, vmem),
+        scratch_shapes=[
+            dma((parts - 1,)),
+            dma((parts - 1,)),
+            dma((lines - 1,)),
+            dma((lines - 1,)),
+            dma((lines,)),
+            dma((lines,)),
+        ],
+        compiler_params=pltpu.CompilerParams(collective_id=0, has_side_effects=True),
+        cost_estimate=pl.CostEstimate(flops=0, bytes_accessed=80_000_000, transcendentals=0),
+    )(layer_in, weights)
+
+
+def end_kernel(
+    owners,
+    parts,
+    g_ref,
+    d_ref,
+    g_out,
+    d_out,
+    pair_in,
+    line_out,
+    line_in,
+    total,
+    d_send,
+    d_recv,
+    p_send,
+    p_recv,
+    l_send,
+    l_recv,
+    s_send,
+    s_recv,
+):
+    line, side, lines, me, line_peers, pair, seq_peers = places(owners, parts)
+    greet(line_peers + [pair] + seq_peers)
+    block = d_ref.shape[1] // parts
+    order = list(range(1, lines)) + [0]
+    paired = {}
+    for k in order:
+        owner = ((line + k) % lines) * 2
+        paired[k] = remote(
+            g_ref.at[owner + 1 - side], pair_in.at[k], p_send.at[k], p_recv.at[k], pair
+        )
+    inputs = []
+    for k, peer in enumerate(seq_peers):
+        start = pl.multiple_of(((me + k + 1) % parts) * block, block)
+        piece = d_ref.at[:, pl.ds(start, block), :]
+        inputs.append(remote(piece, d_out.at[k], d_send.at[k], d_recv.at[k], peer))
+    lined = []
+    for k in range(1, lines):
+        paired[k].wait_recv()
+        owner = ((line + k) % lines) * 2
+        both = g_ref[owner + side].astype(jnp.float32) + pair_in[k].astype(jnp.float32)
+        line_out[k - 1] = both.astype(line_out.dtype)
+        lined.append(
+            remote(
+                line_out.at[k - 1],
+                line_in.at[k - 1],
+                l_send.at[k - 1],
+                l_recv.at[k - 1],
+                line_peers[k - 1],
+            )
+        )
+    paired[0].wait_recv()
+    held = g_ref[line * 2 + side].astype(jnp.float32) + pair_in[0].astype(jnp.float32)
+    for k in range(1, lines):
+        lined[k - 1].wait_recv()
+        held = held + line_in[k - 1].astype(jnp.float32)
+    total[...] = held.astype(total.dtype)
+    g_out[me] = held.astype(g_out.dtype)
+    shared = []
+    for k, peer in enumerate(seq_peers):
+        shared.append(remote(total, g_out.at[me], s_send.at[k], s_recv.at[k], peer))
+    for k in range(lines):
+        paired[k].wait_send()
+    for copy in lined:
+        copy.wait_send()
+    for copy in inputs + shared:
+        copy.wait()
+
+
+def scatter_end(grads, partial, owners, parts):
+    rows, cols = grads.shape
+    own, lines = rows // owners, owners // 2
+    seqs_here, full_len, width = partial.shape
+    block = full_len // parts
+    vmem = pl.BlockSpec(memory_space=pltpu.VMEM)
+    dma = pltpu.SemaphoreType.DMA
+    dtype = grads.dtype
+    return pl.pallas_call(
+        functools.partial(end_kernel, owners, parts),
+        out_shape=(
+            jax.ShapeDtypeStruct((parts, own, cols), dtype),
+            jax.ShapeDtypeStruct((parts - 1, seqs_here, block, width), partial.dtype),
+        ),
+        in_specs=[vmem, vmem],
+        out_specs=(vmem, vmem),
+        scratch_shapes=[
+            pltpu.VMEM((lines, own, cols), dtype),
+            pltpu.VMEM((lines - 1, own, cols), dtype),
+            pltpu.VMEM((lines - 1, own, cols), dtype),
+            pltpu.VMEM((own, cols), dtype),
+            dma((parts - 1,)),
+            dma((parts - 1,)),
+            dma((lines,)),
+            dma((lines,)),
+            dma((lines - 1,)),
+            dma((lines - 1,)),
+            dma((parts - 1,)),
+            dma((parts - 1,)),
+        ],
+        compiler_params=pltpu.CompilerParams(collective_id=1, has_side_effects=True),
+        cost_estimate=pl.CostEstimate(flops=0, bytes_accessed=80_000_000, transcendentals=0),
+    )(grads.reshape(owners, own, cols), partial)
 
 
 def gather_seq(array):
@@ -403,10 +595,10 @@
         axis=1,
     )
     small = jnp.pad(small, ((0, 0), (0, 128 - small.shape[1])))
-    tokens = gather_seq(layer_in)
-    early = lax.all_gather(
-        jnp.concatenate([out_weight, small, qkv_mine], axis=1), "dp", axis=0, tiled=True
-    )
+    tokens, early = gather_start(
+        layer_in, jnp.concatenate([out_weight, small, qkv_mine], axis=1), owners, parts
+    )
+    early = flat(early)
     late = lax.all_gather(
         jnp.concatenate([up_mine, down_mine], axis=1), "dp", axis=0, tiled=True
     )
@@ -507,14 +699,16 @@
         ]
     )
     small_grads = jnp.pad(small_grads, ((0, 128 - small_grads.shape[0]), (0, 0))).T
-    early_grads = scatter_dp(
-        jnp.concatenate([small_grads, qkv_weight_grad, out_weight_grad], axis=1)
-    )
-    d_in = flat(scatter_seq(dot(d_qkv, w_qkv.T).reshape(seqs_here, full_len, width)))
-    grad_in = d_first + d_in
+    d_in = dot(d_qkv, w_qkv.T)
+    early_all, d_others = scatter_end(
+        jnp.concatenate([small_grads, qkv_weight_grad, out_weight_grad], axis=1).astype(bf16),
+        d_in.reshape(seqs_here, full_len, width).astype(bf16),
+        owners,
+        parts,
+    )
+    grad_in = d_first + here(d_in) + flat(jnp.sum(d_others.astype(f32), axis=0))
 
     late_all = lax.all_gather(late_grads, "seq", axis=0)
-    early_all = lax.all_gather(early_grads, "seq", axis=0)
     up_owned = late_all[:, :, :hidden_part].reshape(parts, own, owners, unit)
     up_owned = up_owned.transpose(1, 2, 0, 3).reshape(own, hidden).astype(f32)
     down_owned = late_all[:, :, hidden_part:].reshape(parts * unit, width).astype(f32)

time: 334 us -> 283 us (0.85)
  waiting for transfers between devices: 171 us -> 39 us
  Pallas kernels: 0 us -> 92.1 us
  blocking collectives: 43.8 us -> 24.2 us
  matrix products: 28.8 us -> 34.1 us
  other arithmetic: 19.5 us -> 23.7 us
    pallas_call x0 -> x2, Pallas kernels: none -> 92.1 us  [the longest x1 58.6 us: gather_start(): pl.pallas_call(functools.partial(start_kernel, owners, parts), out_shape=...]
    reduce_scatter x2 -> x1, waiting for transfers between devices: 79.5 us -> 25.9 us  [scatter_dp(): lax.psum_scatter(grads.astype(jnp.bfloat16), 'dp', scatter_dimension=0, t...]
    all_gather x1 -> x0, waiting for transfers between devices: 41.4 us -> none  [on_device(): lax.all_gather(jnp.concatenate([out_weight, small, qkv_mine], axis=1), 'd...]
    all_gather x1, waiting for transfers between devices: 30.7 us -> 0.01 us  [on_device(): lax.all_gather(jnp.concatenate([up_mine, down_mine], axis=1), 'dp', axis=...]
    all_gather x3 -> x2, blocking collectives: 26.3 us -> 16.1 us  [gather_seq(): return lax.all_gather(array, 'seq', axis=1, tiled=True)]
    all_gather x1 -> x0, blocking collectives: 8.54 us -> none  [on_device(): early_all = lax.all_gather(early_grads, 'seq', axis=0)]
    dot_general x12, matrix products: 17.8 us -> 23 us  [dot(): return jnp.dot(a, b, preferred_element_type=f32)]
    all_to_all x3 -> x2, waiting for transfers between devices: 16.9 us -> 13 us  [scatter_seq(): got = lax.all_to_all(pieces, 'seq', 1, 1)]
  transfers between devices with their start and end apart: 8 -> 5, of which waited for: 7 -> 3; matrix products, arithmetic and copies ran while one was open for 17% -> 24% of each run, Pallas kernels for 0% -> 33%
where the time goes in v2:
time: 283 us; the launch traced here: 281 us
  Pallas kernels  92.1 us (33%)
  local copies, waits for them, and re-layouts  45.2 us (16%)
  waiting for transfers between devices  39 us (14%)
  matrix products  34.1 us (12%)
  blocking collectives  24.2 us (9%)
  other arithmetic  23.7 us (8%)
  between operations  14.6 us (5%)
  starting transfers between devices  8.5 us (3%)
    pallas_call x1, Pallas kernels, gather_start(): pl.pallas_call(functools.partial(start_kernel, owners, parts), out_shape=...  58.6 us
    pallas_call x1, Pallas kernels, scatter_end(): pl.pallas_call(functools.partial(end_kernel, owners, parts), out_shape=(j...  33.5 us
    reduce_scatter x1, waiting for transfers between devices, scatter_dp(): lax.psum_scatter(grads.astype(jnp.bfloat16), 'dp', scatter_dimension=0, t...  25.9 us
    dot_general x12, matrix products, dot(): return jnp.dot(a, b, preferred_element_type=f32)  23 us
    all_gather x2, blocking collectives, gather_seq(): return lax.all_gather(array, 'seq', axis=1, tiled=True)  16.1 us
    all_to_all x2, waiting for transfers between devices, scatter_seq(): got = lax.all_to_all(pieces, 'seq', 1, 1)  13 us
    all_to_all x2, starting transfers between devices, scatter_seq(): got = lax.all_to_all(pieces, 'seq', 1, 1)  8.38 us
    all_gather x1, blocking collectives, on_device(): attended = lax.all_gather(mixed, 'seq', axis=2, tiled=True)  8.1 us
  transfers between devices with their start and end apart: 5, of which 3 were waited for; matrix products, arithmetic and copies ran while one was open for 24% of the time, Pallas kernels for 33%

profile of v2, /device:TPU:0, one launch (start us, length us, event | category | flops | bytes accessed | tf_op | source)
XLA Modules:
  0.0 281.3 jit_solution(14647783163667875765)
XLA Ops:
  7.3 2.4 reshape.718
  9.6 1.2 dynamic-slice_reduce_fusion
  14.3 58.6 %shard_map.271 = (bf16[2,256,768]{2,1,0:T(8,128)(2,1)}, bf16[8,96,1472]{2,1,0:T(8,128)(2,1)}) custom-call(bf16[2,64,768]{2,1,0:T(8,128)(2,1)} %x_ref.1, bf16[96,1472]{1,0:T(8,128)(2,1)} %fusion.51.w_ref), custom_call_target="tpu_custom_call" | custom-call | bytes 80000000 | tf_op jit(solution)/shard_map/pallas_call | solution.py:398
  75.0 2.1 fusion.15
  79.1 8.1 %all_gather.18 = bf16[2,256,768]{1,0,2:T(2,128)(2,1)} all-gather(bf16[2,256,192]{1,0,2:T(2,128)(2,1)S(1)} %copy.151), channel_id=1, replica_groups=mesh['dp'=8,'seq'=4] {'seq'}, dimensions={2}, use_global_device_ids=true | all-gather | bytes 983040 | tf_op jit(solution)/shard_map/all_gather | solution.py:631
  87.2 2.2 copy.152
  89.5 2.4 fusion.82
  92.5 2.0 multiply_add_fusion
  94.5 3.9 %multiply_convert_fusion.1 = (bf16[512,768]{1,0:T(8,128)(2,1)S(1)}, f32[512,768]{1,0:T(8,128)}) fusion(f32[768]{0:T(1024)S(1)} %copy-done.29, bf16[768,1536]{1,0:T(8,128)(2,1)} %all-gather.4.cloned.1.call-done, f32[512,768]{1,0:T(8,128)} %get-tuple-element.51), kind=kOutput, calls=%fused_computation.13 | convolution fusion | flops 606732288 | bytes 5114880 | tf_op jit(solution)/shard_map/dot_general | solution.py:570
  100.3 4.2 %all-to-all-start = ((bf16[2,4,64,768]{3,2,0,1:T(8,128)(2,1)}), bf16[2,4,64,768]{3,2,0,1:T(8,128)(2,1)}, u32[]{:S(2)}, u32[]{:S(2)}) async-start(bf16[2,4,64,768]{3,2,0,1:T(8,128)(2,1)} %copy.154), calls=%async_computation | async-start | bytes 1572864 | tf_op jit(solution)/shard_map/all_to_all | solution.py:530
  104.6 11.6 %all-to-all-done = bf16[2,4,64,768]{3,2,0,1:T(8,128)(2,1)} async-done(((bf16[2,4,64,768]{3,2,0,1:T(8,128)(2,1)}), bf16[2,4,64,768]{3,2,0,1:T(8,128)(2,1)}, u32[]{:S(2)}, u32[]{:S(2)}) %all-to-all-start) | async-done | bytes 786464 | tf_op jit(solution)/shard_map/all_to_all | solution.py:530
  116.2 1.3 convert_reduce_fusion.1
  117.5 1.1 fusion.77
  119.1 1.6 fusion.45
  120.7 8.2 %all_gather.20 = bf16[2,256,768]{2,1,0:T(8,128)(2,1)S(1)} all-gather(bf16[2,64,768]{2,1,0:T(8,128)(2,1)S(1)} %get-tuple-element.55), channel_id=1, replica_groups=mesh['dp'=8,'seq'=4] {'seq'}, dimensions={1}, use_global_device_ids=true | all-gather | bytes 983040 | tf_op jit(solution)/shard_map/all_gather | solution.py:523
  130.6 1.7 fusion.83
  134.0 1.6 pad_maximum_fusion
  135.6 4.3 %copy.175 = bf16[768,1536]{1,0:T(8,128)(2,1)} copy(bf16[768,1536]{0,1:T(8,128)(2,1)} %pad_maximum_fusion) | data formatting | bytes 4718592
  139.9 2.3 convolution_convert_fusion.3
  143.2 4.2 %all-to-all-start.1 = ((bf16[2,4,64,768]{3,2,0,1:T(8,128)(2,1)}), bf16[2,4,64,768]{3,2,0,1:T(8,128)(2,1)}, u32[]{:S(2)}, u32[]{:S(2)}) async-start(bf16[2,4,64,768]{3,2,0,1:T(8,128)(2,1)} %copy.155), calls=%async_computation.1 | async-start | bytes 1572864 | tf_op jit(solution)/shard_map/all_to_all | solution.py:530
  147.4 1.3 rsqrt.28
  148.7 2.4 slice.131
  151.0 1.2 copy.164
  152.2 2.3 copy.162
  157.7 1.4 all-to-all-done.1
  159.0 1.3 convert_reduce_fusion
  160.3 2.0 multiply_reduce_fusion.2
  162.3 1.1 fusion.75
  163.5 7.9 %all_gather.21 = bf16[2,256,768]{2,1,0:T(8,128)(2,1)S(1)} all-gather(bf16[2,64,768]{2,1,0:T(8,128)(2,1)S(1)} %convert_element_type.155), channel_id=1, replica_groups=mesh['dp'=8,'seq'=4] {'seq'}, dimensions={1}, use_global_device_ids=true | all-gather | bytes 983040 | tf_op jit(solution)/shard_map/all_gather | solution.py:523
  171.4 2.1 convolution_convert_fusion.7
  174.4 1.6 fusion.59
  176.0 3.4 %fusion.19 = bf16[1,2,3,256,64]{3,4,2,1,0:T(8,128)(2,1)} fusion(f32[2,3,256,256]{2,3,1,0:T(8,128)} %fusion.59, f32[2,3,256,256]{2,3,1,0:T(8,128)S(1)} %get-tuple-element.64, f32[2,3,256]{2,1,0:T(4,128)S(1)} %log_add_fusion, bf16[3,2,3,256,64]{3,4,2,1,0:T(8,128)(2,1)S(1)} %bitcast.125), kind=kOutput, calls=%fused_computation.38 | convolution fusion | flops 53184256 | bytes 6701056 | tf_op jit(solution)/shard_map/shbl,shbd->shld/dot_general | solution.py:677
  179.4 1.1 fusion.55
  180.5 4.2 %fusion.79 = (bf16[3,64]{1,0:T(4,128)(2,1)S(1)}, bf16[1,2,3,256,64]{3,4,2,1,0:T(8,128)(2,1)}, bf16[1,2,3,256,64]{3,4,2,1,0:T(8,128)(2,1)}, bf16[3,64]{1,0:T(4,128)(2,1)}) fusion(f32[2,3,256,64]{2,3,1,0:T(8,128)} %fusion.55, f32[2,3,256,256]{2,3,1,0:T(8,128)} %fusion.59, f32[2,3,256,256]{2,3,1,0:T(8,128)S(1)} %get-tuple-element.64, ...), kind=kOutput, calls=%fused_computation.153 | convolution fusion | flops 53478784 | bytes 7291648 | tf_op jit(solution)/shard_map/shbl,shld->shbd/dot_general | solution.py:676
  184.7 1.1 maximum_bitcast_fusion
  186.6 1.2 reshape.733
  189.4 2.1 convolution_convert_fusion.2
  191.5 1.4 pad_maximum_fusion.1.g_ref
  192.9 25.9 %reduce-scatter.4.cloned.1.call-done = bf16[96,1536]{1,0:T(8,128)(2,1)} async-done(((bf16[768,1536]{1,0:T(8,128)(2,1)}), bf16[96,1536]{1,0:T(8,128)(2,1)}) %reduce-scatter.4.cloned.1.call-update) | async-done | bytes 294928 | tf_op jit(solution)/shard_map/reduce_scatter | solution.py:535
  218.9 3.4 %fusion.84 = (bf16[2,256,768]{2,1,0:T(8,128)(2,1)}, f32[2,256,768]{2,1,0:T(8,128)}) fusion(bf16[2,256,576]{1,2,0:T(8,128)(2,1)S(1)} %bitcast.135, bf16[768,1472]{1,0:T(8,128)(2,1)} %bitcast.134), kind=kOutput, calls=%fused_computation.158 | convolution fusion | flops 453378048 | bytes 3932160 | tf_op jit(solution)/shard_map/dot_general | solution.py:570
  222.3 33.5 %shard_map.272 = (bf16[4,96,896]{2,1,0:T(8,128)(2,1)}, bf16[3,2,64,768]{3,2,1,0:T(8,128)(2,1)}) custom-call(bf16[8,96,896]{2,1,0:T(8,128)(2,1)} %pad_maximum_fusion.1.g_ref, bf16[2,256,768]{2,1,0:T(8,128)(2,1)} %get-tuple-element.71.d_ref), custom_call_target="tpu_custom_call" | custom-call | bytes 80000000 | tf_op jit(solution)/shard_map/pallas_call | solution.py:495
  255.8 1.1 slice_convert_fusion.1
  258.1 1.7 reshape.725
  263.0 1.8 add_add_fusion.1
  264.9 2.2 fusion.78
  267.8 2.2 copy.170
  269.9 3.7 %reshape.727 = f32[96,3072]{1,0:T(8,128)} reshape(f32[96,8,4,96]{3,2,1,0:T(4,128)} %copy.170) | data formatting | bytes 2359296 | tf_op jit(solution)/shard_map/convert_element_type | solution.py:713
  273.6 1.1 bitcast_convert_fusion
  (182 shorter events, 26.1 us)
Async XLA Ops:
  7.2 4.0 %copy-start = (bf16[384,768]{1,0:T(8,128)(2,1)S(1)}, bf16[384,768]{1,0:T(8,128)(2,1)}, u32[]{:S(2)}) copy-start(bf16[384,768]{1,0:T(8,128)(2,1)} %param.27) | copy-start | bytes 1769476
  7.2 87.3 %all-gather.4.cloned.1.call-start = ((), (), s32[]{:S(2)}) async-start(), calls=%async_computation.3 | async-start | bytes 2654208 | tf_op jit(solution)/shard_map/all_gather | solution.py:602
  7.2 4.7 %copy-start.9 = (bf16[96,2304]{1,0:T(8,128)(2,1)S(1)}, bf16[96,2304]{1,0:T(8,128)(2,1)}, u32[]{:S(2)}) copy-start(bf16[96,2304]{1,0:T(8,128)(2,1)} %param.18) | copy-start | bytes 1327108
  10.9 2.0 copy-start.43
  10.9 2.1 copy-start.33
  10.9 2.1 copy-start.34
  10.9 2.0 copy-start.35
  10.9 2.0 copy-start.36
  10.9 2.0 copy-start.37
  11.0 2.0 copy-start.38
  11.0 2.0 copy-start.39
  11.0 2.0 copy-start.40
  11.2 2.4 copy-start.11
  78.9 10.6 %copy-start.30 = (f32[768]{0:T(1024)S(1)}, f32[768]{0:T(1024)}, u32[]{:S(2)}) copy-start(f32[768]{0:T(1024)} %get-tuple-element.35) | copy-start | bytes 9220
  92.2 2.3 copy-start.13
  92.5 2.0 copy-start.29
  94.5 4.0 %copy-start.41 = (bf16[768,1536]{1,0:T(8,128)(2,1)S(1)}, bf16[768,1536]{1,0:T(8,128)(2,1)}, u32[]{:S(2)}) copy-start(bf16[768,1536]{1,0:T(8,128)(2,1)} %all-gather.4.cloned.1.call-done) | copy-start | bytes 7077892
  100.3 15.9 %all-to-all-start = ((bf16[2,4,64,768]{3,2,0,1:T(8,128)(2,1)}), bf16[2,4,64,768]{3,2,0,1:T(8,128)(2,1)}, u32[]{:S(2)}, u32[]{:S(2)}) async-start(bf16[2,4,64,768]{3,2,0,1:T(8,128)(2,1)} %copy.154), calls=%async_computation | async-start | bytes 1572864 | tf_op jit(solution)/shard_map/all_to_all | solution.py:530
  104.5 14.4 %copy-start.3 = (bf16[2,64,768]{2,1,0:T(8,128)(2,1)S(1)}, bf16[2,64,768]{2,1,0:T(8,128)(2,1)}, u32[]{:S(2)}) copy-start(bf16[2,64,768]{2,1,0:T(8,128)(2,1)} %param.31) | copy-start | bytes 589828
  104.5 114.3 %reduce-scatter.4.cloned.1.call-start = ((), (), s32[]{:S(2)}) async-start(), calls=%async_computation.5 | async-start | bytes 2654208 | tf_op jit(solution)/shard_map/reduce_scatter | solution.py:535
  116.2 2.9 %copy-start.15 = (f32[768]{0:T(1024)S(1)}, f32[768]{0:T(1024)}, u32[]{:S(2)}) copy-start(f32[768]{0:T(1024)} %get-tuple-element.30) | copy-start | bytes 9220
  118.6 10.3 %copy-start.12 = (f32[2,64]{1,0:T(2,128)}, f32[2,64]{1,0:T(2,128)S(1)}, u32[]{:S(2)}) copy-start(f32[2,64]{1,0:T(2,128)S(1)} %broadcast_multiply_fusion.5) | copy-start | bytes 1540
  118.6 10.3 %copy-start.47 = (bf16[512,768]{1,0:T(8,128)(2,1)S(1)}, bf16[512,768]{1,0:T(8,128)(2,1)}, u32[]{:S(2)}) copy-start(bf16[512,768]{1,0:T(8,128)(2,1)} %copy-done.46) | copy-start | bytes 2359300
  118.8 10.0 %copy-start.14 = (f32[2,64]{1,0:T(2,128)}, f32[2,64]{1,0:T(2,128)S(1)}, u32[]{:S(2)}) copy-start(f32[2,64]{1,0:T(2,128)S(1)} %add_rsqrt_fusion.1) | copy-start | bytes 1540
  119.1 9.8 %copy-start.21 = (f32[2,64]{1,0:T(2,128)}, f32[2,64]{1,0:T(2,128)S(1)}, u32[]{:S(2)}) copy-start(f32[2,64]{1,0:T(2,128)S(1)} %broadcast_multiply_fusion.3) | copy-start | bytes 1540
  119.1 9.8 %copy-start.22 = (f32[2,64]{1,0:T(2,128)}, f32[2,64]{1,0:T(2,128)S(1)}, u32[]{:S(2)}) copy-start(f32[2,64]{1,0:T(2,128)S(1)} %broadcast_multiply_fusion.4) | copy-start | bytes 1540
  120.7 9.1 %copy-start.45 = (f32[512,768]{1,0:T(8,128)S(1)}, f32[512,768]{1,0:T(8,128)}, u32[]{:S(2)}) copy-start(f32[512,768]{1,0:T(8,128)} %get-tuple-element.68) | copy-start | bytes 4718596
  130.6 2.6 copy-start.2
  143.2 15.9 %all-to-all-start.1 = ((bf16[2,4,64,768]{3,2,0,1:T(8,128)(2,1)}), bf16[2,4,64,768]{3,2,0,1:T(8,128)(2,1)}, u32[]{:S(2)}, u32[]{:S(2)}) async-start(bf16[2,4,64,768]{3,2,0,1:T(8,128)(2,1)} %copy.155), calls=%async_computation.1 | async-start | bytes 1572864 | tf_op jit(solution)/shard_map/all_to_all | solution.py:530
  147.4 117.5 %all-gather.6.cloned.1.call-start = ((), (), s32[]{:S(2)}) async-start(), calls=%async_computation.4 | async-start | bytes 1474560 | tf_op jit(solution)/shard_map/all_gather | solution.py:711
  152.2 3.0 %copy-start.27 = (f32[2,256,1]{1,0,2:T(2,128)S(1)}, f32[2,256,1]{1,0,2:T(2,128)}, u32[]{:S(2)}) copy-start(f32[2,256,1]{1,0,2:T(2,128)} %rsqrt.28) | copy-start | bytes 6148
  152.2 3.7 %copy-start.26 = (bf16[768]{0:T(1024)(128)(2,1)S(1)}, bf16[768]{0:T(1024)(128)(2,1)}, u32[]{:S(2)}) copy-start(bf16[768]{0:T(1024)(128)(2,1)} %get-tuple-element.26) | copy-start | bytes 4612
  152.2 4.3 %copy-start.25 = (bf16[768]{0:T(1024)(128)(2,1)S(1)}, bf16[768]{0:T(1024)(128)(2,1)}, u32[]{:S(2)}) copy-start(bf16[768]{0:T(1024)(128)(2,1)} %get-tuple-element.25) | copy-start | bytes 4612
  152.2 4.9 %copy-start.31 = (bf16[768]{0:T(1024)(128)(2,1)S(1)}, bf16[768]{0:T(1024)(128)(2,1)}, u32[]{:S(2)}) copy-start(bf16[768]{0:T(1024)(128)(2,1)} %get-tuple-element.69) | copy-start | bytes 4612
  159.0 3.3 %copy-start.28 = (f32[2,64]{1,0:T(2,128)S(1)}, f32[2,64]{1,0:T(2,128)}, u32[]{:S(2)}) copy-start(f32[2,64]{1,0:T(2,128)} %fusion.66) | copy-start | bytes 1540
  180.5 4.2 %copy-start.10 = (bf16[1,2,3,256,64]{3,4,2,1,0:T(8,128)(2,1)S(1)}, bf16[1,2,3,256,64]{3,4,2,1,0:T(8,128)(2,1)}, u32[]{:S(2)}) copy-start(bf16[1,2,3,256,64]{3,4,2,1,0:T(8,128)(2,1)} %fusion.19) | copy-start | bytes 589828
  185.8 1.9 copy-start.32
  185.8 2.1 copy-start.24
  185.9 2.1 copy-start.23
  185.9 2.7 copy-start.17
  185.9 2.7 copy-start.18
  185.9 2.7 copy-start.19
  185.9 2.7 copy-start.20
  186.5 2.3 copy-start.4
  258.1 1.7 copy-start.6
  259.8 3.2 %copy-start.8 = (bf16[3,2,64,768]{3,2,1,0:T(8,128)(2,1)S(1)}, bf16[3,2,64,768]{3,2,1,0:T(8,128)(2,1)}, u32[]{:S(2)}) copy-start(bf16[3,2,64,768]{3,2,1,0:T(8,128)(2,1)} %get-tuple-element.21) | copy-start | bytes 1769476
  269.9 3.7 %copy-start.5 = (bf16[4,96,768]{2,1,0:T(8,128)(2,1)S(1)}, bf16[4,96,768]{2,1,0:T(8,128)(2,1)}, u32[]{:S(2)}) copy-start(bf16[4,96,768]{2,1,0:T(8,128)(2,1)} %get-tuple-element.53) | copy-start | bytes 1769476
  269.9 4.8 %copy-start.1 = (bf16[384,768]{1,0:T(8,128)(2,1)S(1)}, bf16[384,768]{1,0:T(8,128)(2,1)}, u32[]{:S(2)}) copy-start(bf16[384,768]{1,0:T(8,128)(2,1)} %param.27) | copy-start | bytes 1769476
  (5 other events, 4.8 us)
Sparse Core Ops, SparseCore 0:
  12.1 75.7 all-gather.3
  140.0 78.7 reduce-scatter.3
  220.4 21.8 all-gather.5

commit v3 on v2

--- a/solution.py
+++ b/solution.py
@@ -519,16 +519,49 @@
     )(grads.reshape(owners, own, cols), partial)
 
 
-def gather_seq(array):
-    return lax.all_gather(array, "seq", axis=1, tiled=True)
-
-
-def scatter_seq(partial):
-    seqs_here, full_len, width = partial.shape
-    count = lax.axis_size("seq")
-    pieces = partial.astype(jnp.bfloat16).reshape(seqs_here, count, full_len // count, width)
-    got = lax.all_to_all(pieces, "seq", 1, 1)
-    return jnp.sum(got.astype(jnp.float32), axis=1)
+def seq_kernel(parts, kind, x_ref, out_ref, send, recv):
+    me = lax.axis_index("seq")
+    peers = [{"seq": (me + k) % parts} for k in range(1, parts)]
+    greet(peers)
+    copies = []
+    if kind == "deal":
+        block = x_ref.shape[1] // parts
+        for k, peer in enumerate(peers):
+            start = pl.multiple_of(((me + k + 1) % parts) * block, block)
+            piece = x_ref.at[:, pl.ds(start, block), :]
+            copies.append(remote(piece, out_ref.at[k], send.at[k], recv.at[k], peer))
+    else:
+        block = x_ref.shape[1]
+        if kind == "rows":
+            slot = (slice(None), pl.ds(pl.multiple_of(me * block, block), block))
+        else:
+            slot = (me,)
+        for k, peer in enumerate(peers):
+            copies.append(remote(x_ref, out_ref.at[slot], send.at[k], recv.at[k], peer))
+        out_ref[slot] = x_ref[...]
+    for copy in copies:
+        copy.wait()
+
+
+def seq_call(array, parts, kind, number):
+    seqs_here, rows, width = array.shape
+    if kind == "deal":
+        shape = (parts - 1, seqs_here, rows // parts, width)
+    elif kind == "rows":
+        shape = (seqs_here, rows * parts, width)
+    else:
+        shape = (parts, seqs_here, rows, width)
+    vmem = pl.BlockSpec(memory_space=pltpu.VMEM)
+    dma = pltpu.SemaphoreType.DMA
+    return pl.pallas_call(
+        functools.partial(seq_kernel, parts, kind),
+        out_shape=jax.ShapeDtypeStruct(shape, array.dtype),
+        in_specs=[vmem],
+        out_specs=vmem,
+        scratch_shapes=[dma((parts - 1,)), dma((parts - 1,))],
+        compiler_params=pltpu.CompilerParams(collective_id=number, has_side_effects=True),
+        cost_estimate=pl.CostEstimate(flops=0, bytes_accessed=15_000_000, transcendentals=0),
+    )(array)
 
 
 def scatter_dp(grads):
@@ -628,8 +661,8 @@
     probs = probs_exact.astype(bf16)
     mixed = jnp.einsum("shbl,shld->shbd", probs, values, preferred_element_type=f32)
     mixed = mixed.astype(bf16).transpose(0, 2, 1, 3).reshape(seqs_here, full_len, cols)
-    attended = lax.all_gather(mixed, "seq", axis=2, tiled=True)
-    attended_flat = flat(attended)
+    attended = seq_call(mixed, parts, "slots", 2)
+    attended_flat = attended.transpose(1, 2, 0, 3).reshape(seqs_here * full_len, width)
     first_sum = tokens_flat.astype(f32) + dot(attended_flat, w_out) + b_out
     first_norm, normed_all, inverse_all = layer_norm(first_sum, gain_one, shift_one)
 
@@ -639,9 +672,15 @@
 
     normed_one, inverse_one = here(normed_all), here(inverse_all)
     first_round = first_norm.astype(bf16)
+
+    def deal(partial, number):
+        pieces = partial.astype(bf16).reshape(seqs_here, full_len, width)
+        others = seq_call(pieces, parts, "deal", number)
+        return here(partial) + flat(jnp.sum(others.astype(f32), axis=0))
+
     inner = dot(first_round, w_up) + b_up
     activated = gelu_exact(inner).astype(bf16)
-    down = flat(scatter_seq(dot(activated, w_down).reshape(seqs_here, full_len, width)))
+    down = deal(dot(activated, w_down), 3)
     second_sum = here(first_norm) + down + b_down
     layer_out, normed_two, inverse_two = layer_norm(second_sum, gain_two, shift_two)
 
@@ -649,21 +688,25 @@
     ffn_gain_grad = jnp.sum(upstream * normed_two, axis=0)
     ffn_shift_grad = jnp.sum(upstream, axis=0)
     d_second = norm_back(upstream, normed_two, inverse_two, gain_two)
-    d_second_all = flat(gather_seq(d_second.astype(bf16).reshape(seqs_here, block, width)))
+    d_second_all = flat(
+        seq_call(d_second.astype(bf16).reshape(seqs_here, block, width), parts, "rows", 4)
+    )
     down_bias_grad = jnp.sum(d_second, axis=0)
     d_inner = dot(d_second_all, w_down.T) * gelu_slope(inner)
     d_inner_round = d_inner.astype(bf16)
-    d_up = flat(scatter_seq(dot(d_inner_round, w_up.T).reshape(seqs_here, full_len, width)))
+    d_up = deal(dot(d_inner_round, w_up.T), 5)
     down_weight_grad = dot(activated.T, d_second_all)
     up_weight_grad = dot(first_round.T, d_inner_round)
     up_bias_grad = jnp.sum(d_inner, axis=0)
-    late_grads = scatter_dp(jnp.concatenate([up_weight_grad, down_weight_grad], axis=1))
+    late_grads = scatter_dp(up_weight_grad)
     d_first_norm = d_second + d_up
     attn_gain_grad = jnp.sum(d_first_norm * normed_one, axis=0)
     attn_shift_grad = jnp.sum(d_first_norm, axis=0)
     d_first = norm_back(d_first_norm, normed_one, inverse_one, gain_one)
     out_bias_grad = jnp.sum(d_first, axis=0)
-    d_first_all = flat(gather_seq(d_first.astype(bf16).reshape(seqs_here, block, width)))
+    d_first_all = flat(
+        seq_call(d_first.astype(bf16).reshape(seqs_here, block, width), parts, "rows", 6)
+    )
     out_weight_grad = dot(
         attended_flat.T, lax.dynamic_slice_in_dim(d_first_all, me * cols, cols, 1)
     )
@@ -701,7 +744,9 @@
     small_grads = jnp.pad(small_grads, ((0, 128 - small_grads.shape[0]), (0, 0))).T
     d_in = dot(d_qkv, w_qkv.T)
     early_all, d_others = scatter_end(
-        jnp.concatenate([small_grads, qkv_weight_grad, out_weight_grad], axis=1).astype(bf16),
+        jnp.concatenate(
+            [down_weight_grad, small_grads, qkv_weight_grad, out_weight_grad], axis=1
+        ).astype(bf16),
         d_in.reshape(seqs_here, full_len, width).astype(bf16),
         owners,
         parts,
@@ -709,9 +754,10 @@
     grad_in = d_first + here(d_in) + flat(jnp.sum(d_others.astype(f32), axis=0))
 
     late_all = lax.all_gather(late_grads, "seq", axis=0)
-    up_owned = late_all[:, :, :hidden_part].reshape(parts, own, owners, unit)
+    down_owned = early_all[:, :, :width].reshape(parts * unit, width).astype(f32)
+    early_all = early_all[:, :, width:]
+    up_owned = late_all.reshape(parts, own, owners, unit)
     up_owned = up_owned.transpose(1, 2, 0, 3).reshape(own, hidden).astype(f32)
-    down_owned = late_all[:, :, hidden_part:].reshape(parts * unit, width).astype(f32)
     small_owned = early_all[:, :, :128].astype(f32)
     sums = jnp.sum(small_owned, axis=0).T
     up_bias_owned = small_owned[:, :, 8].reshape(parts * unit)

time: 283 us -> 328 us (1.16)
  Pallas kernels: 92.1 us -> 197 us
  waiting for transfers between devices: 39 us -> 0.04 us
  blocking collectives: 24.2 us -> 8.11 us
  starting transfers between devices: 8.5 us -> 0.08 us
  matrix products: 34.1 us -> 42.1 us
  local copies, waits for them, and re-layouts: 45.2 us -> 39.8 us
    pallas_call x0 -> x5, Pallas kernels: none -> 65.7 us  [seq_call(): pl.pallas_call(functools.partial(seq_kernel, parts, kind), out_shape=jax....]
    pallas_call x1, Pallas kernels: 33.5 us -> 72.2 us  [scatter_end(): pl.pallas_call(functools.partial(end_kernel, owners, parts), out_shape=(j...]
    reduce_scatter x1, waiting for transfers between devices: 25.9 us -> 0.01 us  [scatter_dp(): lax.psum_scatter(grads.astype(jnp.bfloat16), 'dp', scatter_dimension=0, t...]
    all_gather x3 -> x1, blocking collectives: 24.2 us -> 8.11 us  [on_device(): late_all = lax.all_gather(late_grads, 'seq', axis=0)]
    all_to_all x2 -> x0, waiting for transfers between devices: 13 us -> none  [scatter_seq(): got = lax.all_to_all(pieces, 'seq', 1, 1)]
    all_to_all x2 -> x0, starting transfers between devices: 8.38 us -> none  [scatter_seq(): got = lax.all_to_all(pieces, 'seq', 1, 1)]
    dot_general x12, matrix products: 23 us -> 29.2 us  [dot(): return jnp.dot(a, b, preferred_element_type=f32)]
    unnamed x99 -> x107, local copies, waits for them, and re-layouts: 7.39 us -> 1.54 us
  transfers between devices with their start and end apart: 5 -> 2, of which waited for: 3 -> 0; matrix products, arithmetic and copies ran while one was open for 24% -> 15% of each run, Pallas kernels for 33% -> 44%
where the time goes in v3:
time: 328 us; the launch traced here: 326 us
  Pallas kernels  197 us (60%)
  matrix products  42.1 us (13%)
  local copies, waits for them, and re-layouts  39.8 us (12%)
  other arithmetic  24.7 us (8%)
  between operations  14.9 us (5%)
  blocking collectives  8.11 us (2%)
    pallas_call x1, Pallas kernels, scatter_end(): pl.pallas_call(functools.partial(end_kernel, owners, parts), out_shape=(j...  72.2 us
    pallas_call x5, Pallas kernels, seq_call(): pl.pallas_call(functools.partial(seq_kernel, parts, kind), out_shape=jax....  65.7 us
    pallas_call x1, Pallas kernels, gather_start(): pl.pallas_call(functools.partial(start_kernel, owners, parts), out_shape=...  58.7 us
    dot_general x12, matrix products, dot(): return jnp.dot(a, b, preferred_element_type=f32)  29.2 us
    all_gather x1, blocking collectives, on_device(): late_all = lax.all_gather(late_grads, 'seq', axis=0)  8.11 us
  transfers between devices with their start and end apart: 2, of which 0 were waited for; matrix products, arithmetic and copies ran while one was open for 15% of the time, Pallas kernels for 44%

profile of v3, /device:TPU:0, one launch (start us, length us, event | category | flops | bytes accessed | tf_op | source)
XLA Modules:
  0.0 326.4 jit_solution(3734720954021938841)
XLA Ops:
  7.4 2.4 reshape.726
  9.8 1.2 dynamic-slice_reduce_fusion
  14.4 58.7 %shard_map.271 = (bf16[2,256,768]{2,1,0:T(8,128)(2,1)}, bf16[8,96,1472]{2,1,0:T(8,128)(2,1)}) custom-call(bf16[2,64,768]{2,1,0:T(8,128)(2,1)} %x_ref.1, bf16[96,1472]{1,0:T(8,128)(2,1)} %fusion.53.w_ref), custom_call_target="tpu_custom_call" | custom-call | bytes 80000000 | tf_op jit(solution)/shard_map/pallas_call | solution.py:398
  74.1 2.4 slice.131
  77.6 1.9 fusion.15
  82.2 14.3 %shard_map.272 = bf16[4,2,256,192]{3,2,1,0:T(8,128)(2,1)} custom-call(bf16[2,256,192]{2,1,0:T(8,128)(2,1)} %copy.149.x_ref), custom_call_target="tpu_custom_call" | custom-call | bytes 15000000 | tf_op jit(solution)/shard_map/pallas_call | solution.py:556
  96.5 2.6 copy.150
  99.4 3.8 %fusion.79 = (f32[512]{0:T(512)S(1)}, f32[512,768]{1,0:T(8,128)}) fusion(f32[768]{0:T(1024)S(1)} %get-tuple-element.35, bf16[512,768]{0,1:T(8,128)(2,1)S(1)} %bitcast.139, bf16[768,1472]{1,0:T(8,128)(2,1)} %bitcast.149, bf16[512,768]{1,0:T(8,128)(2,1)} %bitcast.153), kind=kOutput, calls=%fused_computation.150 | convolution fusion | flops 605552128 | bytes 4330496 | tf_op jit(solution)/shard_map/dot_general | solution.py:603
  103.2 1.8 multiply_reduce_fusion.1
  105.6 1.2 copy.159
  107.5 2.9 multiply_add_fusion
  110.4 3.4 %multiply_convert_fusion.1 = (bf16[512,768]{1,0:T(8,128)(2,1)S(1)}, f32[512,768]{1,0:T(8,128)}) fusion(f32[768]{0:T(1024)S(1)} %copy-done.39, bf16[768,1536]{1,0:T(8,128)(2,1)} %all-gather.3.cloned.1.call-done, f32[512,768]{1,0:T(8,128)S(1)} %get-tuple-element.51), kind=kOutput, calls=%fused_computation.10 | convolution fusion | flops 606732288 | bytes 5114880 | tf_op jit(solution)/shard_map/dot_general | solution.py:603
  113.9 2.2 fusion.80
  116.1 12.9 %shard_map.273 = bf16[3,2,64,768]{3,2,1,0:T(8,128)(2,1)} custom-call(bf16[2,256,768]{2,1,0:T(8,128)(2,1)} %bitcast.143), custom_call_target="tpu_custom_call" | custom-call | bytes 15000000 | tf_op jit(solution)/shard_map/pallas_call | solution.py:556
  129.0 1.2 convert_reduce_fusion.2
  130.3 1.2 fusion.77
  131.9 1.7 fusion.47
  133.6 12.8 %shard_map.274 = bf16[2,256,768]{2,1,0:T(8,128)(2,1)} custom-call(bf16[2,64,768]{2,1,0:T(8,128)(2,1)} %get-tuple-element.53.x_ref), custom_call_target="tpu_custom_call" | custom-call | bytes 15000000 | tf_op jit(solution)/shard_map/pallas_call | solution.py:556
  146.4 3.8 %fusion.82 = (bf16[768]{0:T(1024)(128)(2,1)}, bf16[512,768]{1,0:T(8,128)(2,1)S(1)}) fusion(f32[512,768]{1,0:T(8,128)} %get-tuple-element.66, bf16[512,768]{1,0:T(8,128)(2,1)} %bitcast.157, bf16[768,1536]{1,0:T(8,128)(2,1)} %all-gather.3.cloned.1.call-done), kind=kOutput, calls=%fused_computation.153 | convolution fusion | flops 608304384 | bytes 4326912 | tf_op jit(solution)/shard_map/dot_general | solution.py:603
  150.3 2.2 fusion.81
  152.5 12.9 %shard_map.275 = bf16[3,2,64,768]{3,2,1,0:T(8,128)(2,1)} custom-call(bf16[2,256,768]{2,1,0:T(8,128)(2,1)} %bitcast.142), custom_call_target="tpu_custom_call" | custom-call | bytes 15000000 | tf_op jit(solution)/shard_map/pallas_call | solution.py:556
  165.4 1.2 convert_reduce_fusion.1
  166.6 2.1 multiply_reduce_fusion.2
  168.8 1.1 fusion.76
  170.7 12.8 %shard_map.276 = bf16[2,256,768]{2,1,0:T(8,128)(2,1)} custom-call(bf16[2,64,768]{2,1,0:T(8,128)(2,1)} %convert_element_type.150.x_ref), custom_call_target="tpu_custom_call" | custom-call | bytes 15000000 | tf_op jit(solution)/shard_map/pallas_call | solution.py:556
  183.5 2.3 convolution_convert_fusion.5
  185.8 1.7 reshape.735
  187.5 2.1 fusion.57
  189.6 2.5 fusion.61
  192.1 3.4 %fusion.19 = bf16[1,2,3,256,64]{3,4,2,1,0:T(8,128)(2,1)} fusion(f32[2,3,256,256]{2,3,1,0:T(8,128)} %fusion.61, f32[2,3,256,256]{2,3,1,0:T(8,128)S(1)} %get-tuple-element.62, f32[2,3,256]{2,1,0:T(4,128)S(1)} %log_add_fusion, bf16[3,2,3,256,64]{3,4,2,1,0:T(8,128)(2,1)} %bitcast.136), kind=kOutput, calls=%fused_computation.34 | convolution fusion | flops 53184256 | bytes 6701056 | tf_op jit(solution)/shard_map/shbl,shbd->shld/dot_general | solution.py:720
  195.5 4.0 %convert_bitcast_fusion.2 = (bf16[1,2,3,256,64]{3,4,2,1,0:T(8,128)(2,1)}, bf16[3,64]{1,0:T(4,128)(2,1)S(1)}, bf16[3,64]{1,0:T(4,128)(2,1)}, bf16[1,2,3,256,64]{3,4,2,1,0:T(8,128)(2,1)}) fusion(f32[2,3,256,64]{2,3,1,0:T(8,128)S(1)} %copy-done.24, f32[2,3,256,256]{2,3,1,0:T(8,128)} %fusion.61, f32[2,3,256,256]{2,3,1,0:T(8,128)S(1)} %get-tuple-element.62, ...), kind=kOutput, calls=%fused_computation.99 | convolution fusion | flops 53478784 | bytes 7291648 | tf_op jit(solution)/shard_map/shbl,shld->shbd/dot_general | solution.py:719
  199.5 1.3 maximum_bitcast_fusion
  200.8 1.4 copy.160
  203.0 1.8 convolution_convert_fusion
  206.7 1.2 reshape.748
  207.9 1.5 convolution_convert_fusion.3
  209.4 2.0 convolution_convert_fusion.1
  212.3 2.9 concatenate.20.g_ref
  215.2 3.4 %fusion.83 = (bf16[2,256,768]{2,1,0:T(8,128)(2,1)}, f32[2,256,768]{2,1,0:T(8,128)}) fusion(bf16[2,256,576]{1,2,0:T(8,128)(2,1)S(1)} %bitcast.151, bf16[768,1472]{1,0:T(8,128)(2,1)} %bitcast.150), kind=kOutput, calls=%fused_computation.154 | convolution fusion | flops 453378048 | bytes 3932160 | tf_op jit(solution)/shard_map/dot_general | solution.py:603
  218.6 72.2 %shard_map.277 = (bf16[4,96,1664]{2,1,0:T(8,128)(2,1)}, bf16[3,2,64,768]{3,2,1,0:T(8,128)(2,1)}) custom-call(bf16[8,96,1664]{2,1,0:T(8,128)(2,1)} %concatenate.20.g_ref, bf16[2,256,768]{2,1,0:T(8,128)(2,1)} %get-tuple-element.73.d_ref), custom_call_target="tpu_custom_call" | custom-call | bytes 80000000 | tf_op jit(solution)/shard_map/pallas_call | solution.py:495
  290.8 1.1 slice.120
  294.2 1.7 reshape.737
  295.9 1.1 convert_bitcast_fusion
  302.0 1.8 add_add_fusion.1
  303.8 1.1 bitcast_convert_fusion
  304.9 8.1 %all-gather = bf16[384,768]{1,0:T(8,128)(2,1)S(1)} all-gather(bf16[96,768]{1,0:T(8,128)(2,1)} %reduce-scatter.2.cloned.1.call-done), channel_id=2, replica_groups=mesh['dp'=8,'seq'=4] {'seq'}, dimensions={0}, use_global_device_ids=true | all-gather | bytes 737280 | tf_op jit(solution)/shard_map/all_gather | solution.py:756
  313.8 2.2 copy.165
  315.9 3.6 %reshape.739 = f32[96,3072]{1,0:T(8,128)} reshape(f32[96,8,4,96]{3,2,1,0:T(4,128)} %copy.165) | data formatting | bytes 2359296 | tf_op jit(solution)/shard_map/convert_element_type | solution.py:760
  (183 shorter events, 22.1 us)
Async XLA Ops:
  7.2 4.0 %copy-start = (bf16[384,768]{1,0:T(8,128)(2,1)S(1)}, bf16[384,768]{1,0:T(8,128)(2,1)}, u32[]{:S(2)}) copy-start(bf16[384,768]{1,0:T(8,128)(2,1)} %param.27) | copy-start | bytes 1769476
  7.2 103.2 %all-gather.3.cloned.1.call-start = ((), (), s32[]{:S(2)}) async-start(), calls=%async_computation.1 | async-start | bytes 2654208 | tf_op jit(solution)/shard_map/all_gather | solution.py:635
  7.3 4.8 %copy-start.50 = (bf16[384]{0:T(512)(128)(2,1)S(1)}, bf16[384]{0:T(512)(128)(2,1)}, u32[]{:S(2)}) copy-start(bf16[384]{0:T(512)(128)(2,1)} %param.26) | copy-start | bytes 2308
  7.3 4.9 %copy-start.42 = (bf16[96]{0:T(256)(128)(2,1)S(1)}, bf16[96]{0:T(256)(128)(2,1)}, u32[]{:S(2)}) copy-start(bf16[96]{0:T(256)(128)(2,1)} %param.19) | copy-start | bytes 580
  7.3 4.9 %copy-start.43 = (bf16[96]{0:T(256)(128)(2,1)S(1)}, bf16[96]{0:T(256)(128)(2,1)}, u32[]{:S(2)}) copy-start(bf16[96]{0:T(256)(128)(2,1)} %param.20) | copy-start | bytes 580
  7.3 4.9 %copy-start.44 = (bf16[96]{0:T(256)(128)(2,1)S(1)}, bf16[96]{0:T(256)(128)(2,1)}, u32[]{:S(2)}) copy-start(bf16[96]{0:T(256)(128)(2,1)} %param.22) | copy-start | bytes 580
  7.3 4.9 %copy-start.45 = (bf16[96]{0:T(256)(128)(2,1)S(1)}, bf16[96]{0:T(256)(128)(2,1)}, u32[]{:S(2)}) copy-start(bf16[96]{0:T(256)(128)(2,1)} %param.23) | copy-start | bytes 580
  7.3 4.9 %copy-start.46 = (bf16[96]{0:T(256)(128)(2,1)S(1)}, bf16[96]{0:T(256)(128)(2,1)}, u32[]{:S(2)}) copy-start(bf16[96]{0:T(256)(128)(2,1)} %param.24) | copy-start | bytes 580
  7.3 4.9 %copy-start.47 = (bf16[96]{0:T(256)(128)(2,1)S(1)}, bf16[96]{0:T(256)(128)(2,1)}, u32[]{:S(2)}) copy-start(bf16[96]{0:T(256)(128)(2,1)} %param.28) | copy-start | bytes 580
  7.3 4.9 %copy-start.48 = (bf16[96]{0:T(256)(128)(2,1)S(1)}, bf16[96]{0:T(256)(128)(2,1)}, u32[]{:S(2)}) copy-start(bf16[96]{0:T(256)(128)(2,1)} %param.29) | copy-start | bytes 580
  7.3 4.9 %copy-start.49 = (bf16[96]{0:T(256)(128)(2,1)S(1)}, bf16[96]{0:T(256)(128)(2,1)}, u32[]{:S(2)}) copy-start(bf16[96]{0:T(256)(128)(2,1)} %param.30) | copy-start | bytes 580
  7.3 5.1 %copy-start.23 = (bf16[96,2304]{1,0:T(8,128)(2,1)S(1)}, bf16[96,2304]{1,0:T(8,128)(2,1)}, u32[]{:S(2)}) copy-start(bf16[96,2304]{1,0:T(8,128)(2,1)} %param.18) | copy-start | bytes 1327108
  11.3 2.4 copy-start.25
  12.0 292.9 %reduce-scatter.2.cloned.1.call-start = ((), (), s32[]{:S(2)}) async-start(), calls=%async_computation.2 | async-start | bytes 1327104 | tf_op jit(solution)/shard_map/reduce_scatter | solution.py:568
  74.1 3.5 %copy-start.19 = (bf16[2,256,768]{2,1,0:T(8,128)(2,1)S(1)}, bf16[2,256,768]{2,1,0:T(8,128)(2,1)}, u32[]{:S(2)}) copy-start(bf16[2,256,768]{2,1,0:T(8,128)(2,1)} %get-tuple-element.19) | copy-start | bytes 2359300
  99.3 3.8 %copy-start.5 = (bf16[96,8,2,256]{3,1,2,0:T(8,128)(2,1)}, bf16[96,8,2,256]{3,1,2,0:T(8,128)(2,1)S(1)}, u32[]{:S(2)}) copy-start(bf16[96,8,2,256]{3,1,2,0:T(8,128)(2,1)S(1)} %copy.175) | copy-start | bytes 2359300
  103.1 1.9 copy-start.11
  103.1 2.5 copy-start.20
  103.1 3.7 %copy-start.27 = (f32[512]{0:T(512)}, f32[512]{0:T(512)S(1)}, u32[]{:S(2)}) copy-start(f32[512]{0:T(512)S(1)} %broadcast_multiply_fusion) | copy-start | bytes 6148
  105.0 2.5 copy-start.28
  107.5 2.9 copy-start.39
  110.4 3.5 %copy-start.15 = (bf16[768,1536]{1,0:T(8,128)(2,1)S(1)}, bf16[768,1536]{1,0:T(8,128)(2,1)}, u32[]{:S(2)}) copy-start(bf16[768,1536]{1,0:T(8,128)(2,1)} %all-gather.3.cloned.1.call-done) | copy-start | bytes 7077892
  113.9 2.3 copy-start.9
  129.0 2.7 copy-start.12
  129.0 2.9 copy-start.30
  131.4 2.2 copy-start.26
  131.6 1.9 copy-start.29
  131.9 1.7 copy-start.32
  131.9 1.7 copy-start.33
  146.4 3.8 %copy-start.16 = (bf16[768,1536]{1,0:T(8,128)(2,1)S(1)}, bf16[768,1536]{1,0:T(8,128)(2,1)}, u32[]{:S(2)}) copy-start(bf16[768,1536]{1,0:T(8,128)(2,1)} %all-gather.3.cloned.1.call-done) | copy-start | bytes 7077892
  150.3 2.2 copy-start.7
  165.4 3.4 %copy-start.38 = (f32[2,64]{1,0:T(2,128)S(1)}, f32[2,64]{1,0:T(2,128)}, u32[]{:S(2)}) copy-start(f32[2,64]{1,0:T(2,128)} %fusion.68) | copy-start | bytes 1540
  169.9 17.5 %copy-start.2 = (f32[2,64,768]{2,1,0:T(8,128)}, f32[2,64,768]{2,1,0:T(8,128)S(1)}, u32[]{:S(2)}) copy-start(f32[2,64,768]{2,1,0:T(8,128)S(1)} %get-tuple-element.47) | copy-start | bytes 1179652
  187.5 2.1 copy-start.17
  192.1 3.4 %copy-start.24 = (f32[2,3,256,64]{2,3,1,0:T(8,128)S(1)}, f32[2,3,256,64]{2,3,1,0:T(8,128)}, u32[]{:S(2)}) copy-start(f32[2,3,256,64]{2,3,1,0:T(8,128)} %fusion.57) | copy-start | bytes 1179652
  199.5 3.6 %copy-start.8 = (bf16[512,768]{1,0:T(8,128)(2,1)S(1)}, bf16[512,768]{1,0:T(8,128)(2,1)}, u32[]{:S(2)}) copy-start(bf16[512,768]{1,0:T(8,128)(2,1)} %copy-done.7) | copy-start | bytes 2359300
  203.0 1.9 copy-start.10
  204.9 0.9 copy-start.34
  204.9 0.9 copy-start.40
  204.9 1.5 copy-start.31
  204.9 1.8 copy-start.13
  205.0 2.9 copy-start.6
  209.4 2.0 copy-start.18
  209.4 2.0 copy-start.21
  212.3 2.9 copy-start.14
  295.9 6.0 %copy-start.22 = (bf16[3,2,64,768]{3,2,1,0:T(8,128)(2,1)S(1)}, bf16[3,2,64,768]{3,2,1,0:T(8,128)(2,1)}, u32[]{:S(2)}) copy-start(bf16[3,2,64,768]{3,2,1,0:T(8,128)(2,1)} %get-tuple-element.21) | copy-start | bytes 1769476
  297.0 4.9 %copy-start.3 = (f32[2,64,768]{2,1,0:T(8,128)S(1)}, f32[2,64,768]{2,1,0:T(8,128)}, u32[]{:S(2)}) copy-start(f32[2,64,768]{2,1,0:T(8,128)} %copy-done.2) | copy-start | bytes 1179652
  313.8 5.8 %copy-start.1 = (bf16[384,768]{1,0:T(8,128)(2,1)S(1)}, bf16[384,768]{1,0:T(8,128)(2,1)}, u32[]{:S(2)}) copy-start(bf16[384,768]{1,0:T(8,128)(2,1)} %param.27) | copy-start | bytes 1769476
  (6 other events, 4.7 us)
Sparse Core Ops, SparseCore 0:
  12.2 75.7 all-gather.2
  209.5 84.2 reduce-scatter.1
